TPU v7x, 256 devices: a whole 4x4x8 slice. The times are simulated.
256 devices in a mesh: pipe: 4 (over y), rows: 64 (over x, z, core).
Axes of the slice: x: 4, y: 4, z: 8, core: 2. Of those that a mesh axis runs over, the one named last changes fastest.
Arguments:
- features: bfloat16 [128, 65536], P('pipe', 'rows'), may hold values from 0 to 16
- weights: bfloat16 [8, 1024, 64, 256], P('pipe', 'rows'), may hold values from -0.5 to 0.5
- bias: bfloat16 [8, 65536], P('pipe', 'rows'), may hold values from -2 to 2
- layout: int32 [8, 4096], P('pipe'), may hold values from 0 to 1023, as said below
Outputs:
- activations: bfloat16 [128, 65536], P('pipe', 'rows')
Inputs may be any that keep to these rules, and one draw needn't show every extreme that they name: `layout`: for every layer and every index of rows, the 64 slots of that index's 16 output blocks read blocks held by exactly 32 distinct indices of rows (index = block // 16), exactly 2 slots from each of them.
All inputs are finite; a program needn't handle non-finite values.
Results may differ from a plain program's by a relative error of at most 0.013.
Values may be sent and summed in bfloat16 or wider, within the bound.
A program may use at most 64 MiB of HBM per device.

v0:
```python
import jax
import jax.numpy as jnp
from jax import lax
from jax.sharding import PartitionSpec as P

BLOCK = 64
K = 4
MICRO = 8


clamp_top = 32.0


def from_behind(block, axis, distance):
    devices = range(lax.axis_size(axis))
    route = [(i - distance, i) for i in devices if i - distance in devices]
    return lax.ppermute(block, axis, route)


def spread(value, axis, root):
    mine = lax.axis_index(axis) == root
    return lax.psum(jnp.where(mine, value, jnp.zeros_like(value)), axis)


def make_tables(layout_row, my_row, row_devs, blocks_dev, capacity):
    slot_count = layout_row.shape[0] // row_devs
    layout_grid = layout_row.reshape(row_devs, slot_count)
    owners = layout_grid // blocks_dev
    local_idx = layout_grid % blocks_dev
    before = jnp.arange(slot_count)[None, :] < jnp.arange(slot_count)[:, None]
    same_owner = owners[:, :, None] == owners[:, None, :]
    slot_rank = jnp.sum(same_owner & before[None, :, :], axis=2)
    is_mine = owners == my_row
    rank_onehot = (slot_rank[:, :, None] == jnp.arange(capacity)[None, None, :]) & is_mine[
        :, :, None
    ]
    local_onehot = local_idx[:, :, None] == jnp.arange(blocks_dev)[None, None, :]
    chooser = jnp.einsum(
        "dic,dib->dcb", rank_onehot.astype(jnp.float32), local_onehot.astype(jnp.float32)
    ).astype(jnp.bfloat16)
    own_owner = lax.dynamic_index_in_dim(owners, my_row, 0, keepdims=False)
    own_rank = lax.dynamic_index_in_dim(slot_rank, my_row, 0, keepdims=False)
    flat_idx = own_owner * capacity + own_rank
    picker = (flat_idx[:, None] == jnp.arange(row_devs * capacity)[None, :]).astype(jnp.bfloat16)
    return (chooser, picker)


def apply_layer(features_now, chooser, picker, weight_now, bias_now, row_devs, capacity):
    rows_now = features_now.shape[0]
    blocks_dev = chooser.shape[2]
    block_len = weight_now.shape[1]
    blocks = features_now.reshape(rows_now, blocks_dev, block_len)
    outgoing = jnp.einsum("dcb,mbf->dcmf", chooser, blocks, preferred_element_type=jnp.float32)
    outgoing = outgoing.astype(jnp.bfloat16).reshape(row_devs, capacity * rows_now * block_len)
    arrived = lax.all_to_all(outgoing, "rows", split_axis=0, concat_axis=0, tiled=True)
    arrived = arrived.reshape(row_devs * capacity, rows_now * block_len)
    gathered = jnp.dot(picker, arrived, preferred_element_type=jnp.float32).astype(jnp.bfloat16)
    gathered = gathered.reshape(blocks_dev, K, rows_now, block_len)
    weight_four = weight_now.reshape(blocks_dev, block_len, K, block_len)
    summed = jnp.einsum("bkmf,bfkg->mbg", gathered, weight_four, preferred_element_type=jnp.float32)
    summed = summed.reshape(rows_now, blocks_dev * block_len)
    summed = summed + bias_now.astype(jnp.float32)[None, :]
    return jnp.clip(jax.nn.relu(summed), 0.0, clamp_top).astype(jnp.bfloat16)


def on_device(features, weights, bias, layout):
    row_devs = lax.axis_size("rows")
    my_row = lax.axis_index("rows")
    pipe_devs = lax.axis_size("pipe")
    my_segment = lax.axis_index("pipe")
    blocks_dev = features.shape[1] // BLOCK
    slot_count = weights.shape[1] * K
    groups_used = min(row_devs, slot_count // 2)
    capacity = slot_count // groups_used
    tables = [
        make_tables(layout[layer_idx], my_row, row_devs, blocks_dev, capacity)
        for layer_idx in range(weights.shape[0])
    ]
    everyone = lax.all_gather(features, "pipe", axis=0, tiled=True)
    micro_rows = everyone.shape[0] // MICRO
    waiting = jnp.zeros((micro_rows, features.shape[1]), jnp.bfloat16)
    finished_list = []
    for moment in range(MICRO + pipe_devs - 1):
        entry_start = min(moment, MICRO - 1) * micro_rows
        entering = everyone[entry_start : entry_start + micro_rows]
        current = jnp.where(my_segment == 0, entering, waiting)
        for layer_idx in range(weights.shape[0]):
            chooser, picker = tables[layer_idx]
            current = apply_layer(
                current, chooser, picker, weights[layer_idx], bias[layer_idx], row_devs, capacity
            )
        if moment >= pipe_devs - 1:
            finished_list.append(current)
        if moment < MICRO + pipe_devs - 2:
            waiting = from_behind(current, "pipe", 1)
    collected = jnp.concatenate(finished_list, axis=0)
    shared = spread(collected, "pipe", pipe_devs - 1)
    return lax.dynamic_slice_in_dim(shared, my_segment * features.shape[0], features.shape[0], 0)


def solution(mesh):
    in_specs = (
        P("pipe", "rows"),
        P("pipe", "rows", None, None),
        P("pipe", "rows"),
        P("pipe", None),
    )
    out_specs = P("pipe", "rows")
    return jax.shard_map(
        on_device, mesh=mesh, in_specs=in_specs, out_specs=out_specs, check_vma=False
    )
```

profile of v0, /device:TPU:24, one launch (start us, length us, event | category | flops | bytes accessed | tf_op | source)
XLA Modules:
  0.0 681.2 jit_solution(14309318953942179070)
XLA Ops:
  6.5 12.5 %all_gather.3 = bf16[128,1024]{1,0:T(8,128)(2,1)S(1)} all-gather(bf16[32,1024]{1,0:T(8,128)(2,1)} %param.4), channel_id=1, replica_groups=mesh['pipe'=4,'rows'=64] {'pipe'}, dimensions={0}, use_global_device_ids=true | all-gather | bytes 327680 | tf_op jit(solution)/shard_map/all_gather | solution.py:79
  20.3 3.7 convert_reduce_fusion.1
  29.1 11.9 %all-to-all-start = ((bf16[64,2,1024]{2,1,0:T(2,128)(2,1)}), bf16[64,2,1024]{2,1,0:T(2,128)(2,1)S(1)}, u32[]{:S(2)}, u32[]{:S(2)}) async-start(bf16[64,2,1024]{2,1,0:T(2,128)(2,1)} %reshape.766), calls=%async_computation | async-start | bytes 524288 | tf_op jit(solution)/shard_map/all_to_all | solution.py:55
  42.1 11.0 %all-to-all-done = bf16[64,2,1024]{2,1,0:T(2,128)(2,1)S(1)} async-done(((bf16[64,2,1024]{2,1,0:T(2,128)(2,1)}), bf16[64,2,1024]{2,1,0:T(2,128)(2,1)S(1)}, u32[]{:S(2)}, u32[]{:S(2)}) %all-to-all-start) | async-done | bytes 262176 | tf_op jit(solution)/shard_map/all_to_all | solution.py:55
  59.9 6.2 all-to-all-start.1
  66.6 11.5 %all-to-all-done.1 = bf16[64,2,1024]{2,1,0:T(2,128)(2,1)S(1)} async-done(((bf16[64,2,1024]{2,1,0:T(2,128)(2,1)}), bf16[64,2,1024]{2,1,0:T(2,128)(2,1)S(1)}, u32[]{:S(2)}, u32[]{:S(2)}) %all-to-all-start.1) | async-done | bytes 262176 | tf_op jit(solution)/shard_map/all_to_all | solution.py:55
  82.3 4.5 collective-permute-done
  87.9 2.3 reduce.36
  90.4 17.8 %all_to_all.220 = bf16[64,2,1024]{2,1,0:T(2,128)(2,1)S(1)} all-to-all(bf16[64,2,1024]{2,1,0:T(2,128)(2,1)S(1)} %reshape.770), channel_id=1, replica_groups=mesh['pipe'=4,'rows'=64] {'rows'}, dimensions={0} | all-to-all | bytes 524288 | tf_op jit(solution)/shard_map/all_to_all | solution.py:55
  114.4 17.8 %all_to_all.221 = bf16[64,2,1024]{2,1,0:T(2,128)(2,1)S(1)} all-to-all(bf16[64,2,1024]{2,1,0:T(2,128)(2,1)S(1)} %reshape.772), channel_id=1, replica_groups=mesh['pipe'=4,'rows'=64] {'rows'}, dimensions={0} | all-to-all | bytes 524288 | tf_op jit(solution)/shard_map/all_to_all | solution.py:55
  136.4 4.5 collective-permute-done.1
  142.0 2.3 reduce.38
  144.5 17.8 %all_to_all.222 = bf16[64,2,1024]{2,1,0:T(2,128)(2,1)S(1)} all-to-all(bf16[64,2,1024]{2,1,0:T(2,128)(2,1)S(1)} %reshape.774), channel_id=1, replica_groups=mesh['pipe'=4,'rows'=64] {'rows'}, dimensions={0} | all-to-all | bytes 524288 | tf_op jit(solution)/shard_map/all_to_all | solution.py:55
  166.0 2.3 reduce.39
  168.5 18.0 %all_to_all.223 = bf16[64,2,1024]{2,1,0:T(2,128)(2,1)S(1)} all-to-all(bf16[64,2,1024]{2,1,0:T(2,128)(2,1)S(1)} %reshape.776), channel_id=1, replica_groups=mesh['pipe'=4,'rows'=64] {'rows'}, dimensions={0} | all-to-all | bytes 524288 | tf_op jit(solution)/shard_map/all_to_all | solution.py:55
  190.6 4.5 collective-permute-done.2
  196.3 2.3 reduce.40
  198.8 17.8 %all_to_all.224 = bf16[64,2,1024]{2,1,0:T(2,128)(2,1)S(1)} all-to-all(bf16[64,2,1024]{2,1,0:T(2,128)(2,1)S(1)} %reshape.778), channel_id=1, replica_groups=mesh['pipe'=4,'rows'=64] {'rows'}, dimensions={0} | all-to-all | bytes 524288 | tf_op jit(solution)/shard_map/all_to_all | solution.py:55
  220.3 2.3 reduce.41
  222.8 18.0 %all_to_all.225 = bf16[64,2,1024]{2,1,0:T(2,128)(2,1)S(1)} all-to-all(bf16[64,2,1024]{2,1,0:T(2,128)(2,1)S(1)} %reshape.780), channel_id=1, replica_groups=mesh['pipe'=4,'rows'=64] {'rows'}, dimensions={0} | all-to-all | bytes 524288 | tf_op jit(solution)/shard_map/all_to_all | solution.py:55
  245.6 4.5 collective-permute-done.3
  251.2 2.3 reduce.42
  253.7 17.8 %all_to_all.226 = bf16[64,2,1024]{2,1,0:T(2,128)(2,1)S(1)} all-to-all(bf16[64,2,1024]{2,1,0:T(2,128)(2,1)S(1)} %reshape.782), channel_id=1, replica_groups=mesh['pipe'=4,'rows'=64] {'rows'}, dimensions={0} | all-to-all | bytes 524288 | tf_op jit(solution)/shard_map/all_to_all | solution.py:55
  277.7 18.2 %all_to_all.227 = bf16[64,2,1024]{2,1,0:T(2,128)(2,1)S(1)} all-to-all(bf16[64,2,1024]{2,1,0:T(2,128)(2,1)S(1)} %reshape.784), channel_id=1, replica_groups=mesh['pipe'=4,'rows'=64] {'rows'}, dimensions={0} | all-to-all | bytes 524288 | tf_op jit(solution)/shard_map/all_to_all | solution.py:55
  300.7 4.5 collective-permute-done.4
  308.8 18.0 %all_to_all.228 = bf16[64,2,1024]{2,1,0:T(2,128)(2,1)S(1)} all-to-all(bf16[64,2,1024]{2,1,0:T(2,128)(2,1)S(1)} %reshape.786), channel_id=1, replica_groups=mesh['pipe'=4,'rows'=64] {'rows'}, dimensions={0} | all-to-all | bytes 524288 | tf_op jit(solution)/shard_map/all_to_all | solution.py:55
  330.5 2.3 reduce.45
  333.0 17.8 %all_to_all.229 = bf16[64,2,1024]{2,1,0:T(2,128)(2,1)S(1)} all-to-all(bf16[64,2,1024]{2,1,0:T(2,128)(2,1)S(1)} %reshape.788), channel_id=1, replica_groups=mesh['pipe'=4,'rows'=64] {'rows'}, dimensions={0} | all-to-all | bytes 524288 | tf_op jit(solution)/shard_map/all_to_all | solution.py:55
  355.5 4.5 collective-permute-done.5
  361.2 2.3 reduce.46
  363.7 17.8 %all_to_all.230 = bf16[64,2,1024]{2,1,0:T(2,128)(2,1)S(1)} all-to-all(bf16[64,2,1024]{2,1,0:T(2,128)(2,1)S(1)} %reshape.790), channel_id=1, replica_groups=mesh['pipe'=4,'rows'=64] {'rows'}, dimensions={0} | all-to-all | bytes 524288 | tf_op jit(solution)/shard_map/all_to_all | solution.py:55
  387.7 17.8 %all_to_all.231 = bf16[64,2,1024]{2,1,0:T(2,128)(2,1)S(1)} all-to-all(bf16[64,2,1024]{2,1,0:T(2,128)(2,1)S(1)} %reshape.792), channel_id=1, replica_groups=mesh['pipe'=4,'rows'=64] {'rows'}, dimensions={0} | all-to-all | bytes 524288 | tf_op jit(solution)/shard_map/all_to_all | solution.py:55
  410.2 4.5 collective-permute-done.6
  418.4 17.8 %all_to_all.232 = bf16[64,2,1024]{2,1,0:T(2,128)(2,1)S(1)} all-to-all(bf16[64,2,1024]{2,1,0:T(2,128)(2,1)S(1)} %reshape.794), channel_id=1, replica_groups=mesh['pipe'=4,'rows'=64] {'rows'}, dimensions={0} | all-to-all | bytes 524288 | tf_op jit(solution)/shard_map/all_to_all | solution.py:55
  442.4 17.8 %all_to_all.233 = bf16[64,2,1024]{2,1,0:T(2,128)(2,1)S(1)} all-to-all(bf16[64,2,1024]{2,1,0:T(2,128)(2,1)S(1)} %reshape.796), channel_id=1, replica_groups=mesh['pipe'=4,'rows'=64] {'rows'}, dimensions={0} | all-to-all | bytes 524288 | tf_op jit(solution)/shard_map/all_to_all | solution.py:55
  464.9 4.5 collective-permute-done.7
  470.6 2.3 reduce.50
  473.1 18.0 %all_to_all.234 = bf16[64,2,1024]{2,1,0:T(2,128)(2,1)S(1)} all-to-all(bf16[64,2,1024]{2,1,0:T(2,128)(2,1)S(1)} %reshape.798), channel_id=1, replica_groups=mesh['pipe'=4,'rows'=64] {'rows'}, dimensions={0} | all-to-all | bytes 524288 | tf_op jit(solution)/shard_map/all_to_all | solution.py:55
  497.2 17.8 %all_to_all.235 = bf16[64,2,1024]{2,1,0:T(2,128)(2,1)S(1)} all-to-all(bf16[64,2,1024]{2,1,0:T(2,128)(2,1)S(1)} %reshape.800), channel_id=1, replica_groups=mesh['pipe'=4,'rows'=64] {'rows'}, dimensions={0} | all-to-all | bytes 524288 | tf_op jit(solution)/shard_map/all_to_all | solution.py:55
  519.8 4.5 collective-permute-done.8
  527.9 18.0 %all_to_all.236 = bf16[64,2,1024]{2,1,0:T(2,128)(2,1)S(1)} all-to-all(bf16[64,2,1024]{2,1,0:T(2,128)(2,1)S(1)} %reshape.802), channel_id=1, replica_groups=mesh['pipe'=4,'rows'=64] {'rows'}, dimensions={0} | all-to-all | bytes 524288 | tf_op jit(solution)/shard_map/all_to_all | solution.py:55
  552.2 17.8 %all_to_all.237 = bf16[64,2,1024]{2,1,0:T(2,128)(2,1)S(1)} all-to-all(bf16[64,2,1024]{2,1,0:T(2,128)(2,1)S(1)} %reshape.804), channel_id=1, replica_groups=mesh['pipe'=4,'rows'=64] {'rows'}, dimensions={0} | all-to-all | bytes 524288 | tf_op jit(solution)/shard_map/all_to_all | solution.py:55
  574.7 4.5 collective-permute-done.9
  580.4 2.3 reduce.54
  582.9 18.1 %all_to_all.238 = bf16[64,2,1024]{2,1,0:T(2,128)(2,1)S(1)} all-to-all(bf16[64,2,1024]{2,1,0:T(2,128)(2,1)S(1)} %reshape.806), channel_id=1, replica_groups=mesh['pipe'=4,'rows'=64] {'rows'}, dimensions={0} | all-to-all | bytes 524288 | tf_op jit(solution)/shard_map/all_to_all | solution.py:55
  607.8 6.0 all-to-all-start.21
  613.9 11.9 %all-to-all-done.21 = bf16[64,2,1024]{2,1,0:T(2,128)(2,1)S(1)} async-done(((bf16[64,2,1024]{2,1,0:T(2,128)(2,1)}), bf16[64,2,1024]{2,1,0:T(2,128)(2,1)S(1)}, u32[]{:S(2)}, u32[]{:S(2)}) %all-to-all-start.21) | async-done | bytes 262176 | tf_op jit(solution)/shard_map/all_to_all | solution.py:55
  629.9 42.6 %all-reduce.2.cloned.1.call-done = bf16[128,1024]{1,0:T(8,128)(2,1)} async-done(((bf16[128,1024]{1,0:T(8,128)(2,1)}), bf16[128,1024]{1,0:T(8,128)(2,1)}) %all-reduce.2.cloned.1.call-update) | async-done | bytes 262160 | tf_op jit(solution)/shard_map/psum | solution.py:22
  (327 shorter events, 140.3 us)
Async XLA Ops:
  25.5 15.6 %copy-start.2 = (bf16[2,1024]{1,0:T(2,128)(2,1)S(1)}, bf16[2,1024]{1,0:T(2,128)(2,1)}, u32[]{:S(2)}) copy-start(bf16[2,1024]{1,0:T(2,128)(2,1)} %param.6) | copy-start | bytes 12292
  25.5 15.7 %copy-start = (bf16[2,16,64,256]{3,2,1,0:T(8,128)(2,1)S(1)}, bf16[2,16,64,256]{3,2,1,0:T(8,128)(2,1)}, u32[]{:S(2)}) copy-start(bf16[2,16,64,256]{3,2,1,0:T(8,128)(2,1)} %param.5) | copy-start | bytes 3145732
  29.1 23.9 %all-to-all-start = ((bf16[64,2,1024]{2,1,0:T(2,128)(2,1)}), bf16[64,2,1024]{2,1,0:T(2,128)(2,1)S(1)}, u32[]{:S(2)}, u32[]{:S(2)}) async-start(bf16[64,2,1024]{2,1,0:T(2,128)(2,1)} %reshape.766), calls=%async_computation | async-start | bytes 524288 | tf_op jit(solution)/shard_map/all_to_all | solution.py:55
  59.9 18.2 %all-to-all-start.1 = ((bf16[64,2,1024]{2,1,0:T(2,128)(2,1)}), bf16[64,2,1024]{2,1,0:T(2,128)(2,1)S(1)}, u32[]{:S(2)}, u32[]{:S(2)}) async-start(bf16[64,2,1024]{2,1,0:T(2,128)(2,1)} %reshape.768), calls=%async_computation.1 | async-start | bytes 524288 | tf_op jit(solution)/shard_map/all_to_all | solution.py:55
  81.0 5.8 collective-permute-start
  135.1 5.8 collective-permute-start.1
  189.3 5.8 collective-permute-start.2
  244.3 5.8 collective-permute-start.3
  299.4 5.8 collective-permute-start.4
  354.2 5.8 collective-permute-start.5
  408.9 5.8 collective-permute-start.6
  463.6 5.8 collective-permute-start.7
  518.5 5.8 collective-permute-start.8
  573.4 5.8 collective-permute-start.9
  607.8 18.0 %all-to-all-start.21 = ((bf16[64,2,1024]{2,1,0:T(2,128)(2,1)}), bf16[64,2,1024]{2,1,0:T(2,128)(2,1)S(1)}, u32[]{:S(2)}, u32[]{:S(2)}) async-start(bf16[64,2,1024]{2,1,0:T(2,128)(2,1)} %reshape.808), calls=%async_computation.21 | async-start | bytes 524288 | tf_op jit(solution)/shard_map/all_to_all | solution.py:55
  613.8 58.6 %all-reduce.2.cloned.1.call-start = ((), (), s32[]{:S(2)}) async-start(), calls=%async_computation.22 | async-start | bytes 524288 | tf_op jit(solution)/shard_map/psum | solution.py:22
  628.2 1.0 copy-start.1
Sparse Core Ops, SparseCore 0:
  630.0 42.4 all-reduce.1
where the time goes:
time: 693 us; the launch traced here: 681 us
  blocking collectives  352 us (51%)
  waiting for transfers between devices  122 us (18%)
  other arithmetic  95.1 us (14%)
  local copies, waits for them, and re-layouts  39.6 us (6%)
  starting transfers between devices  37.1 us (5%)
  matrix products  19.3 us (3%)
  between operations  15.8 us (2%)
    all_to_all x19, blocking collectives, apply_layer(): lax.all_to_all(outgoing, 'rows', split_axis=0, concat_axis=0, tiled=True)  340 us
    all_to_all x44, other arithmetic, apply_layer(): lax.all_to_all(outgoing, 'rows', split_axis=0, concat_axis=0, tiled=True)  86.1 us
    ppermute x10, waiting for transfers between devices, from_behind(): return lax.ppermute(block, axis, route)  45.1 us
    psum x1, waiting for transfers between devices, spread(): return lax.psum(jnp.where(mine, value, jnp.zeros_like(value)), axis)  42.6 us
    all_to_all x3, waiting for transfers between devices, apply_layer(): lax.all_to_all(outgoing, 'rows', split_axis=0, concat_axis=0, tiled=True)  34.4 us
    all_to_all x3, starting transfers between devices, apply_layer(): lax.all_to_all(outgoing, 'rows', split_axis=0, concat_axis=0, tiled=True)  24.2 us
  transfers between devices with their start and end apart: 14, of which 14 were waited for; matrix products, arithmetic and copies ran while one was open for 0% of the time, Pallas kernels for 0%

commit v1 on v0

v1 whole, which is shorter than its diff:
```python
import functools

import jax
import jax.numpy as jnp
from jax import lax
from jax.experimental import pallas as pl
from jax.experimental.pallas import tpu as pltpu
from jax.sharding import PartitionSpec as P

MESH = pl.DeviceIdType.MESH
BLOCK = 64
K = 4
X, Z, C = 4, 8, 2
PIPE = 4
ROWS = X * Z * C
LAYERS = 8
OWN = LAYERS // PIPE
BD = 16
SUBS = 2
CHUNKS = 4
clamp_top = 32.0

NEAR, AHEAD, BACK, FAR = (0, 6), (6, 4), (10, 4), (14, 2)


def place():
    me = lax.axis_index("rows")
    return lax.axis_index("pipe"), me // (Z * C), (me // C) % Z, me % C


def device(dy, dx, dz, dc):
    y, x, z, c = place()
    row = (((x + dx + X) % X) * Z + (z + dz + Z) % Z) * C + (c + dc) % C
    return ((y + dy + PIPE) % PIPE, row)


def offsets():
    found = [(1, 0, 0, 0), (2, 0, 0, 0), (3, 0, 0, 0), (0, 0, 2, 0), (0, 0, -2, 0)]
    for dx in range(X):
        for dc in range(C):
            for dz in (0, 1, -1, 2 if dc == 0 else -2):
                here = (0, dx, dz, dc)
                if here not in found and here != (0, 0, 0, 0):
                    found.append(here)
    return found


def swap_halves(v):
    return pltpu.roll(v, BLOCK, 1)


def kernel(
    feat_ref, w_hbm, bias_ref, lay_ref, out_ref,
    wall, ready, biases, bias_tiles, tabs, stab, cur, stage, land,
    local_sem, tab_send, tab_recv, bias_send, bias_recv, w_send, w_recv,
    hop_send, hop_recv, leaf_send, leaf_recv,
):
    y, x, z, c = place()
    me = (x * Z + z) * C + c
    rs = cur[0][0].shape[2]
    left = lax.broadcasted_iota(jnp.int32, (BD, 128), 1) < BLOCK

    barrier = pltpu.get_barrier_semaphore()
    partners = offsets()
    for dy, dx, dz, dc in partners:
        pl.semaphore_signal(
            barrier, inc=1, device_id=device(-dy, -dx, -dz, -dc), device_id_type=MESH
        )

    own_w = pltpu.make_async_copy(w_hbm, wall.at[pl.ds(OWN * y, OWN)], local_sem.at[0])
    own_w.start()

    def fold(p, carry):
        cols = pl.ds(pl.multiple_of(p * 128, 128), 128)
        low = feat_ref[pl.ds(0, 16), cols].astype(jnp.float32)
        high = feat_ref[pl.ds(16, 16), cols].astype(jnp.float32)
        even = jnp.where(left, low, swap_halves(high)).astype(jnp.bfloat16)
        odd = jnp.where(left, swap_halves(low), high).astype(jnp.bfloat16)
        for s in range(SUBS):
            cur[0][s][0, 2 * p] = even[s * rs : (s + 1) * rs]
            cur[0][s][0, 2 * p + 1] = odd[s * rs : (s + 1) * rs]
        return carry

    lax.fori_loop(0, BD // 2, fold, 0)
    biases[pl.ds(y, 1)] = bias_ref[...].reshape(1, OWN, bias_ref.shape[1])

    lane = lax.broadcasted_iota(jnp.int32, (ROWS // 2, 128), 1)
    slot = lane & 63
    for a in range(OWN):
        entry = lay_ref[a]
        owner = entry >> 4
        key = slot * BD + (entry & 15)
        table = jnp.zeros((ROWS // 2, 128), jnp.int32)
        for q, dz in enumerate((0, -2, 2)):
            source = (x * Z + (z + dz + Z) % Z) * C + c
            for half in range(2):
                hit = (owner == source) & ((lane >> 6) == half)
                first = jnp.min(jnp.where(hit, key, 1 << 20), axis=1, keepdims=True) & 15
                last = jnp.max(jnp.where(hit, key, 0), axis=1, keepdims=True) & 15
                table = jnp.where(lane == 4 * q + 2 * half, first, table)
                table = jnp.where(lane == 4 * q + 2 * half + 1, last, table)
        tabs[y, a, pl.ds(0, ROWS // 2)] = table
    mine = jnp.concatenate(
        [lay_ref[a, pl.ds(x * Z + z, 1), :] for a in range(OWN)]
        + [jnp.zeros((8 - OWN, 128), jnp.int32)],
        axis=0,
    )
    owner = mine >> 4
    spot = lax.broadcasted_iota(jnp.int32, (8, 128), 1) & 63
    rank = jnp.zeros((8, 128), jnp.int32)
    for step in range(1, 64):
        same = (pltpu.roll(owner, step, 1) == owner) & (spot >= step)
        rank = jnp.where(same, 1, rank)
    dx = (x - (owner >> 4) + X) & (X - 1)
    dz = (z - ((owner >> 1) & (Z - 1)) + Z) & (Z - 1)
    dc = (c + owner) & 1
    base = jnp.zeros((8, 128), jnp.int32)
    for d, at in ((0, 0), (2, 2), (6, 4), (1, 6), (3, 8), (7, 10), (5, 12), (4, 14)):
        base = jnp.where(dz == d, at, base)
    where = (dx * 2 + dc) * 16 + base + rank
    for a in range(OWN):
        tabs[y, a, pl.ds(ROWS // 2, 8)] = jnp.broadcast_to(where[a : a + 1], (8, 128))

    pl.semaphore_wait(barrier, len(partners))

    def tab_copy(dy):
        return pltpu.make_async_remote_copy(
            tabs.at[y], tabs.at[y], tab_send, tab_recv,
            device_id=device(dy, 0, 0, 0), device_id_type=MESH,
        )

    def bias_copy(dy):
        return pltpu.make_async_remote_copy(
            biases.at[y], biases.at[y], bias_send, bias_recv,
            device_id=device(dy, 0, 0, 0), device_id_type=MESH,
        )

    def hop(l, s, dz, q):
        return pltpu.make_async_remote_copy(
            cur[l][s].at[0], cur[l][s].at[q], hop_send.at[l, s], hop_recv.at[l, s],
            device_id=device(0, 0, dz, 0), device_id_type=MESH,
        )

    def start_hops(l, s):
        hop(l, s, 2, 1).start()
        hop(l, s, -2, 2).start()

    rows = BD // CHUNKS

    def w_copy(l, chunk, dy, src):
        piece = pl.ds(chunk * rows, rows)
        return pltpu.make_async_remote_copy(
            src.at[piece], wall.at[l, piece], w_send, w_recv.at[l, chunk],
            device_id=device(dy, 0, 0, 0), device_id_type=MESH,
        )

    def w_own(a, dy, order):
        for chunk in order:
            w_copy(OWN * y + a, chunk, dy, w_hbm.at[a]).start()

    def w_wait(l, order):
        for chunk in order:
            w_copy(l, chunk, 1, wall.at[l]).wait_recv()

    def w_pass(l, order, dy):
        for chunk in order:
            w_wait(l, (chunk,))
            w_copy(l, chunk, dy, wall.at[l]).start()

    def at_y(which, act):
        pl.when(y == which)(act)

    first_half, last_half, forward, turned = (0, 1), (2, 3), (0, 1, 2, 3), (2, 3, 0, 1)

    def point(p):
        if p == 0:
            @functools.partial(at_y, 0)
            def _():
                for a in range(OWN):
                    w_own(a, 1, forward)
                    w_own(a, -1, turned)

            @functools.partial(at_y, 1)
            def _():
                for a in range(OWN):
                    w_own(a, -1, turned)

        if p == 1:
            @functools.partial(at_y, 1)
            def _():
                w_pass(0, first_half, 1)
                w_own(0, 1, first_half)

            @functools.partial(at_y, 3)
            def _():
                w_pass(0, last_half, -1)

        if p == 2:
            @functools.partial(at_y, 1)
            def _():
                w_pass(1, first_half, 1)
                w_own(0, 1, last_half)
                w_own(1, 1, forward)

            @functools.partial(at_y, 3)
            def _():
                w_pass(1, last_half, -1)

            @functools.partial(at_y, 0)
            def _():
                w_pass(2, last_half, -1)
                w_pass(3, last_half, -1)

            @functools.partial(at_y, 2)
            def _():
                w_pass(2, first_half, 1)
                for dy in (1, 3, 2):
                    w_own(0, dy, forward)

        if p == 3:
            @functools.partial(at_y, 2)
            def _():
                w_pass(3, first_half, 1)
                for dy in (1, 3, 2):
                    w_own(1, dy, forward)

            @functools.partial(at_y, 3)
            def _():
                for a in range(OWN):
                    for dy in (1, 3, 2):
                        w_own(a, dy, forward)

    def arrive(l):
        own = l // OWN
        for who in range(PIPE):
            dist = (who - own) % PIPE
            order = forward
            if l < 4:
                order = {1: last_half, 2: forward, 3: first_half}.get(dist, ())
            if dist:
                at_y(who, functools.partial(w_wait, l, order))
        if l % OWN == 0:
            at_y(own, own_w.wait)

    def prepare(l):
        keep = lax.broadcasted_iota(jnp.int32, (BLOCK, 128), 1) < BLOCK

        def one(r, carry):
            for p in range(2):
                raw = wall[l, r, :, pl.ds(p * 128, 128)].astype(jnp.float32)
                turn = swap_halves(raw)
                zero = jnp.zeros_like(raw)
                parts = (
                    jnp.where(keep, raw, zero), jnp.where(keep, zero, turn),
                    jnp.where(keep, turn, zero), jnp.where(keep, zero, raw),
                )
                for i, part in enumerate(parts):
                    ready[l, r, pl.ds((p * 4 + i) * BLOCK, BLOCK), :] = part.astype(jnp.bfloat16)
            return carry

        lax.fori_loop(0, BD, one, 0)

        line_left = lax.broadcasted_iota(jnp.int32, (1, 128), 1) < BLOCK

        for p in range(BD // 2):
            row = biases[l // OWN, pl.ds(l % OWN, 1), pl.ds(p * 128, 128)].astype(jnp.float32)
            turn = swap_halves(row)
            bias_tiles[l, pl.ds(2 * p, 1), :] = jnp.where(line_left, row, turn)
            bias_tiles[l, pl.ds(2 * p + 1, 1), :] = jnp.where(line_left, turn, row)

    def leaf(l, s, u, dx, dz, dc, part):
        tiles = pl.ds(u * 16 + part[0], part[1])
        return pltpu.make_async_remote_copy(
            stage.at[l, s, tiles], land[l][s].at[tiles], leaf_send.at[l, s], leaf_recv.at[l, s],
            device_id=device(0, dx, dz, dc), device_id_type=MESH,
        )

    def spread(l, s):
        pltpu.make_async_remote_copy(
            cur[l][s].at[pl.ds(1, 2)], cur[l][s].at[pl.ds(1, 2)], hop_send.at[l, s], hop_recv.at[l, s],
            device_id=device(0, 0, 2, 0), device_id_type=MESH,
        ).wait_recv()

        def column(t, carry):
            dx = (t // 2) ^ 2
            dc = t % 2
            u = dx * 2 + dc
            cc = (c + dc) % C
            xx = ((x + dx) % X) * Z

            def put(at, q, dz):
                for k in range(2):
                    index = stab[l // OWN, l % OWN, xx + (z + dz + Z) % Z, 4 * q + 2 * cc + k]
                    stage[l, s, u * 16 + at + k] = cur[l][s][q, index]

            far = 2 - 4 * dc
            put(14, 1 + dc, far)
            leaf(l, s, u, dx, far, dc, FAR).start()
            put(6, 0, 1)
            put(8, 1, 1)
            leaf(l, s, u, dx, 1, dc, AHEAD).start()
            put(10, 0, -1)
            put(12, 2, -1)
            leaf(l, s, u, dx, -1, dc, BACK).start()
            put(0, 0, 0)
            put(2, 1, 0)
            put(4, 2, 0)

            @pl.when(u > 0)
            def _():
                leaf(l, s, u, dx, 0, dc, NEAR).start()

            return carry

        lax.fori_loop(0, X * C, column, 0)
        for k in range(NEAR[1]):
            land[l][s][k] = stage[l, s, k]

    def gather(l, s):
        tiles = pl.ds(NEAR[1], 8 * 16 - NEAR[1])
        pltpu.make_async_remote_copy(
            stage.at[l, s, tiles], land[l][s].at[tiles], leaf_send.at[l, s], leaf_recv.at[l, s],
            device_id=device(0, 1, 0, 0), device_id_type=MESH,
        ).wait_recv()

    def block_out(l, s, r):
        row = stab.at[l // OWN, l % OWN, ROWS // 2]
        lhs = jnp.concatenate([land[l][s][row[c * 64 + r * K + k]] for k in range(K)], axis=1)
        total = jnp.dot(lhs, ready[l, r], preferred_element_type=jnp.float32)
        total = total + bias_tiles[l, pl.ds(r, 1), :]
        return jnp.minimum(jnp.maximum(total, 0.0), clamp_top)

    def advance(l, s):
        gather(l, s)

        def pair(p, carry):
            for r in range(2):
                cur[l + 1][s][0, 2 * p + r] = block_out(l, s, 2 * p + r).astype(jnp.bfloat16)
            return carry

        lax.fori_loop(0, BD // 2, pair, 0)
        start_hops(l + 1, s)

    def finish(l, s):
        gather(l, s)
        half = left[:rs]

        def pair(p, carry):
            even, odd = block_out(l, s, 2 * p), block_out(l, s, 2 * p + 1)
            cols = pl.ds(pl.multiple_of(p * 128, 128), 128)
            low = jnp.where(half, even, swap_halves(odd))
            high = jnp.where(half, swap_halves(even), odd)
            out_ref[pl.ds(s * rs, rs), cols] = low.astype(jnp.bfloat16)
            out_ref[pl.ds(16 + s * rs, rs), cols] = high.astype(jnp.bfloat16)
            return carry

        lax.fori_loop(0, BD // 2, pair, 0)

    for dy in (2, 1, 3):
        tab_copy(dy).start()
    for s in range(SUBS):
        start_hops(0, s)
    for dy in (1, 2, 3):
        bias_copy(dy).start()
    point(0)
    pltpu.make_async_remote_copy(
        tabs.at[pl.ds(0, 3)], tabs.at[pl.ds(0, 3)], tab_send, tab_recv,
        device_id=device(1, 0, 0, 0), device_id_type=MESH,
    ).wait()
    to_smem = pltpu.make_async_copy(tabs, stab, local_sem.at[1])
    to_smem.start()
    to_smem.wait()

    last = LAYERS - 1
    spread(0, 0)
    spread(0, 1)
    point(1)
    pltpu.make_async_remote_copy(
        biases.at[pl.ds(0, 3)], biases.at[pl.ds(0, 3)], bias_send, bias_recv,
        device_id=device(1, 0, 0, 0), device_id_type=MESH,
    ).wait()
    arrive(0)
    prepare(0)
    for l in range(LAYERS):
        if l < last:
            advance(l, 0)
            spread(l + 1, 0)
            advance(l, 1)
            point(l + 2)
            if l == 0:
                spread(l + 1, 1)
            arrive(l + 1)
            prepare(l + 1)
            if l > 0:
                spread(l + 1, 1)
        else:
            finish(l, 0)
            finish(l, 1)

    for l in range(LAYERS):
        for s in range(SUBS):
            pltpu.make_async_remote_copy(
                cur[l][s].at[pl.ds(0, 2)], cur[l][s].at[pl.ds(0, 2)], hop_send.at[l, s], hop_recv.at[l, s],
                device_id=device(0, 0, 2, 0), device_id_type=MESH,
            ).wait_send()
            tiles = pl.ds(NEAR[1], 8 * 16 - NEAR[1])
            pltpu.make_async_remote_copy(
                stage.at[l, s, tiles], land[l][s].at[tiles], leaf_send.at[l, s], leaf_recv.at[l, s],
                device_id=device(0, 1, 0, 0), device_id_type=MESH,
            ).wait_send()
    for who in range(PIPE):
        n = {0: 4 + 1, 1: 4 + 1, 2: 6 + 1, 3: 6 + 1}[who]

        @functools.partial(at_y, who)
        def _():
            pltpu.make_async_remote_copy(
                wall.at[pl.ds(0, n)], wall.at[pl.ds(0, n)], w_send, w_recv.at[0, 0],
                device_id=device(1, 0, 0, 0), device_id_type=MESH,
            ).wait_send()


def on_device(features, weights, bias, layout):
    rs = 16 // SUBS
    n = bias.shape[1]
    return pl.pallas_call(
        kernel,
        name="sections",
        out_shape=jax.ShapeDtypeStruct(features.shape, jnp.bfloat16),
        in_specs=[
            pl.BlockSpec(memory_space=pltpu.VMEM),
            pl.BlockSpec(memory_space=pl.ANY),
            pl.BlockSpec(memory_space=pltpu.VMEM),
            pl.BlockSpec(memory_space=pltpu.VMEM),
        ],
        out_specs=pl.BlockSpec(memory_space=pltpu.VMEM),
        scratch_shapes=[
            pltpu.VMEM((LAYERS,) + weights.shape[1:], jnp.bfloat16),
            pltpu.VMEM((LAYERS, BD, 2 * K * BLOCK, 2 * BLOCK), jnp.bfloat16),
            pltpu.VMEM((PIPE, OWN, n), jnp.bfloat16),
            pltpu.VMEM((LAYERS, BD, 2 * BLOCK), jnp.float32),
            pltpu.VMEM((PIPE, OWN, ROWS // 2 + 8, 128), jnp.int32),
            pltpu.SMEM((PIPE, OWN, ROWS // 2 + 8, 128), jnp.int32),
            [[pltpu.VMEM((3, BD, rs, 128), jnp.bfloat16)] * SUBS] * LAYERS,
            pltpu.VMEM((LAYERS, SUBS, 128, rs, 128), jnp.bfloat16),
            [[pltpu.VMEM((128, rs, 128), jnp.bfloat16)] * SUBS] * LAYERS,
            pltpu.SemaphoreType.DMA((2,)),
            pltpu.SemaphoreType.DMA,
            pltpu.SemaphoreType.DMA,
            pltpu.SemaphoreType.DMA,
            pltpu.SemaphoreType.DMA,
            pltpu.SemaphoreType.DMA,
            pltpu.SemaphoreType.DMA((LAYERS, CHUNKS)),
            pltpu.SemaphoreType.DMA((LAYERS, SUBS)),
            pltpu.SemaphoreType.DMA((LAYERS, SUBS)),
            pltpu.SemaphoreType.DMA((LAYERS, SUBS)),
            pltpu.SemaphoreType.DMA((LAYERS, SUBS)),
        ],
        compiler_params=pltpu.CompilerParams(
            collective_id=0, has_side_effects=True, vmem_limit_bytes=60 * 1024 * 1024
        ),
    )(features, weights, bias, layout.reshape(OWN, ROWS // 2, 128))


def solution(mesh):
    in_specs = (
        P("pipe", "rows"),
        P("pipe", "rows", None, None),
        P("pipe", "rows"),
        P("pipe", None),
    )
    return jax.shard_map(
        on_device, mesh=mesh, in_specs=in_specs, out_specs=P("pipe", "rows"), check_vma=False
    )
```

time: 693 us -> 134 us (0.19); the launches traced: 681 us -> 133 us
  blocking collectives: 352 us -> 0 us
  Pallas kernels: 0 us -> 131 us
  waiting for transfers between devices: 122 us -> 0 us
  other arithmetic: 95.1 us -> 0 us
  starting transfers between devices: 37.1 us -> 0 us
  local copies, waits for them, and re-layouts: 39.6 us -> 2.85 us
  matrix products: 19.3 us -> 0 us
  between operations: 15.8 us -> 0.01 us
    all_to_all x19 -> x0, blocking collectives: 340 us -> none  [apply_layer(): lax.all_to_all(outgoing, 'rows', split_axis=0, concat_axis=0, tiled=True)]
    pallas_call x0 -> x1, Pallas kernels: none -> 131 us  [on_device(): pl.pallas_call(kernel, name='sections', out_shape=jax.ShapeDtypeStruct(fe...]
    all_to_all x44 -> x0, other arithmetic: 86.1 us -> none  [apply_layer(): lax.all_to_all(outgoing, 'rows', split_axis=0, concat_axis=0, tiled=True)]
    ppermute x10 -> x0, waiting for transfers between devices: 45.1 us -> none  [from_behind(): return lax.ppermute(block, axis, route)]
    psum x1 -> x0, waiting for transfers between devices: 42.6 us -> none  [spread(): return lax.psum(jnp.where(mine, value, jnp.zeros_like(value)), axis)]
    all_to_all x3 -> x0, waiting for transfers between devices: 34.4 us -> none  [apply_layer(): lax.all_to_all(outgoing, 'rows', split_axis=0, concat_axis=0, tiled=True)]
    all_to_all x3 -> x0, starting transfers between devices: 24.2 us -> none  [apply_layer(): lax.all_to_all(outgoing, 'rows', split_axis=0, concat_axis=0, tiled=True)]
    dot_general x68 -> x0, matrix products: 19.3 us -> none  [the longest x22 7.07 us: apply_layer(): jnp.einsum('dcb,mbf->dcmf', chooser, blocks, preferred_element_type=jnp.f...]
  transfers between devices with their start and end apart: 14 -> 0, of which waited for: 14 -> 0; matrix products, arithmetic and copies ran while one was open for 0% -> 0% of each run, Pallas kernels for 0% -> 0%
where the time goes in v1:
time: 134 us; the launch traced here: 133 us
  Pallas kernels  131 us (98%)
  local copies, waits for them, and re-layouts  2.85 us (2%)
    pallas_call x1, Pallas kernels, on_device(): pl.pallas_call(kernel, name='sections', out_shape=jax.ShapeDtypeStruct(fe...  131 us
    unnamed x2, local copies, waits for them, and re-layouts  2.85 us

profile of v1, /device:TPU:24, one launch (start us, length us, event | category | flops | bytes accessed | tf_op | source)
XLA Modules:
  0.0 133.4 jit_solution(14753678583264690262)
XLA Ops:
  0.0 1.4 %copy.7 = s32[1,2,32,128]{3,2,1,0:T(8,128)} copy(s32[1,2,32,128]{3,1,2,0:T(2,128)} %bitcast.5) | data formatting | bytes 65536
  1.4 130.6 %sections.1 = bf16[32,1024]{1,0:T(8,128)(2,1)} custom-call(bf16[32,1024]{1,0:T(8,128)(2,1)} %feat_ref.1, bf16[2,16,64,256]{3,2,1,0:T(8,128)(2,1)} %w_hbm.1, bf16[2,1024]{1,0:T(2,128)(2,1)} %bias_ref.1, s32[2,32,128]{2,1,0:T(8,128)} %bitcast.4), custom_call_target="tpu_custom_call" | custom-call | tf_op jit(solution)/shard_map/sections/pallas_call | solution.py:425
  131.9 1.5 %copy.9 = bf16[32,1024]{1,0:T(8,128)(2,1)} copy(bf16[32,1024]{1,0:T(8,128)(2,1)} %sections.1) | data formatting | bytes 131072

commit v2 on v1

--- a/solution.py
+++ b/solution.py
@@ -20,7 +20,9 @@
 CHUNKS = 4
 clamp_top = 32.0
 
-NEAR, AHEAD, BACK, FAR = (0, 6), (6, 4), (10, 4), (14, 2)
+OWN_PARTS = ((6, 1, (0,)), (10, -1, (0,)), (0, 0, (0,)))
+RELAY_PARTS = ((8, 1, (1,)), (12, -1, (2,)), (2, 0, (1, 2)))
+HERE = 6
 
 
 def place():
@@ -51,13 +53,13 @@
 
 def kernel(
     feat_ref, w_hbm, bias_ref, lay_ref, out_ref,
-    wall, ready, biases, bias_tiles, tabs, stab, cur, stage, land,
-    local_sem, tab_send, tab_recv, bias_send, bias_recv, w_send, w_recv,
+    wall, ready, biases, bias_tiles, tabs, stab, cur, near, stage, land,
+    local_sem, smem_sem, tab_send, tab_recv, bias_send, bias_recv, w_send, w_recv,
     hop_send, hop_recv, leaf_send, leaf_recv,
 ):
     y, x, z, c = place()
     me = (x * Z + z) * C + c
-    rs = cur[0][0].shape[2]
+    rs = cur[0][0].shape[1]
     left = lax.broadcasted_iota(jnp.int32, (BD, 128), 1) < BLOCK
 
     barrier = pltpu.get_barrier_semaphore()
@@ -77,8 +79,8 @@
         even = jnp.where(left, low, swap_halves(high)).astype(jnp.bfloat16)
         odd = jnp.where(left, swap_halves(low), high).astype(jnp.bfloat16)
         for s in range(SUBS):
-            cur[0][s][0, 2 * p] = even[s * rs : (s + 1) * rs]
-            cur[0][s][0, 2 * p + 1] = odd[s * rs : (s + 1) * rs]
+            cur[0][s][2 * p] = even[s * rs : (s + 1) * rs]
+            cur[0][s][2 * p + 1] = odd[s * rs : (s + 1) * rs]
         return carry
 
     lax.fori_loop(0, BD // 2, fold, 0)
@@ -87,7 +89,9 @@
     lane = lax.broadcasted_iota(jnp.int32, (ROWS // 2, 128), 1)
     slot = lane & 63
     for a in range(OWN):
-        entry = lay_ref[a]
+        entry = jnp.concatenate(
+            [lay_ref[pl.ds(a, 1), pl.ds(i * 128, 128)] for i in range(ROWS // 2)], axis=0
+        )
         owner = entry >> 4
         key = slot * BD + (entry & 15)
         table = jnp.zeros((ROWS // 2, 128), jnp.int32)
@@ -101,7 +105,7 @@
                 table = jnp.where(lane == 4 * q + 2 * half + 1, last, table)
         tabs[y, a, pl.ds(0, ROWS // 2)] = table
     mine = jnp.concatenate(
-        [lay_ref[a, pl.ds(x * Z + z, 1), :] for a in range(OWN)]
+        [lay_ref[:, pl.ds(pl.multiple_of((x * Z + z) * 128, 128), 128)]]
         + [jnp.zeros((8 - OWN, 128), jnp.int32)],
         axis=0,
     )
@@ -121,11 +125,12 @@
     for a in range(OWN):
         tabs[y, a, pl.ds(ROWS // 2, 8)] = jnp.broadcast_to(where[a : a + 1], (8, 128))
 
-    pl.semaphore_wait(barrier, len(partners))
+    with jax.named_scope("barrier_wait"):
+        pl.semaphore_wait(barrier, len(partners))
 
     def tab_copy(dy):
         return pltpu.make_async_remote_copy(
-            tabs.at[y], tabs.at[y], tab_send, tab_recv,
+            tabs.at[y], tabs.at[y], tab_send, tab_recv.at[y],
             device_id=device(dy, 0, 0, 0), device_id_type=MESH,
         )
 
@@ -137,13 +142,13 @@
 
     def hop(l, s, dz, q):
         return pltpu.make_async_remote_copy(
-            cur[l][s].at[0], cur[l][s].at[q], hop_send.at[l, s], hop_recv.at[l, s],
+            cur[l][s], near[l][s].at[q], hop_send.at[l, s], hop_recv.at[l, s],
             device_id=device(0, 0, dz, 0), device_id_type=MESH,
         )
 
     def start_hops(l, s):
-        hop(l, s, 2, 1).start()
-        hop(l, s, -2, 2).start()
+        hop(l, s, 2, 0).start()
+        hop(l, s, -2, 1).start()
 
     rows = BD // CHUNKS
 
@@ -172,72 +177,56 @@
 
     first_half, last_half, forward, turned = (0, 1), (2, 3), (0, 1, 2, 3), (2, 3, 0, 1)
 
+    both, ahead, behind = (1, -1), (1,), (-1,)
+    program = (
+        (
+            (0, ("own", 0, both, forward), ("own", 1, both, forward)),
+            (1, ("own", 0, behind, turned), ("own", 1, behind, turned)),
+            (2, ("own", 0, both, forward), ("own", 1, both, forward)),
+            (3, ("own", 0, ahead, forward), ("own", 1, ahead, forward)),
+        ),
+        (
+            (1, ("pass", 0, ahead, first_half), ("own", 0, ahead, forward), ("own", 1, ahead, forward)),
+            (3, ("pass", 0, behind, last_half)),
+        ),
+        (
+            (0, ("pass", 2, behind, last_half), ("pass", 3, behind, last_half)),
+            (2, ("pass", 2, ahead, first_half)),
+            (3, ("pass", 1, behind, forward), ("own", 0, behind, turned), ("own", 1, behind, turned)),
+        ),
+        (
+            (0, ("pass", 6, ahead, first_half), ("pass", 7, ahead, first_half)),
+            (1, ("pass", 4, behind, last_half), ("pass", 5, behind, last_half)),
+            (2, ("pass", 3, ahead, first_half)),
+            (3, ("pass", 4, ahead, first_half), ("pass", 5, ahead, first_half)),
+        ),
+        (
+            (2, ("pass", 6, behind, last_half), ("pass", 7, behind, last_half)),
+        ),
+    )
+
     def point(p):
-        if p == 0:
-            @functools.partial(at_y, 0)
+        for who, *acts in program[p] if p < len(program) else ():
+            @functools.partial(at_y, who)
             def _():
-                for a in range(OWN):
-                    w_own(a, 1, forward)
-                    w_own(a, -1, turned)
-
-            @functools.partial(at_y, 1)
-            def _():
-                for a in range(OWN):
-                    w_own(a, -1, turned)
-
-        if p == 1:
-            @functools.partial(at_y, 1)
-            def _():
-                w_pass(0, first_half, 1)
-                w_own(0, 1, first_half)
-
-            @functools.partial(at_y, 3)
-            def _():
-                w_pass(0, last_half, -1)
-
-        if p == 2:
-            @functools.partial(at_y, 1)
-            def _():
-                w_pass(1, first_half, 1)
-                w_own(0, 1, last_half)
-                w_own(1, 1, forward)
-
-            @functools.partial(at_y, 3)
-            def _():
-                w_pass(1, last_half, -1)
-
-            @functools.partial(at_y, 0)
-            def _():
-                w_pass(2, last_half, -1)
-                w_pass(3, last_half, -1)
-
-            @functools.partial(at_y, 2)
-            def _():
-                w_pass(2, first_half, 1)
-                for dy in (1, 3, 2):
-                    w_own(0, dy, forward)
-
-        if p == 3:
-            @functools.partial(at_y, 2)
-            def _():
-                w_pass(3, first_half, 1)
-                for dy in (1, 3, 2):
-                    w_own(1, dy, forward)
-
-            @functools.partial(at_y, 3)
-            def _():
-                for a in range(OWN):
-                    for dy in (1, 3, 2):
-                        w_own(a, dy, forward)
+                for kind, which, ways, order in acts:
+                    for dy in ways:
+                        if kind == "own":
+                            w_own(which, dy, order)
+                        else:
+                            w_pass(which, order, dy)
 
     def arrive(l):
         own = l // OWN
         for who in range(PIPE):
-            dist = (who - own) % PIPE
-            order = forward
-            if l < 4:
-                order = {1: last_half, 2: forward, 3: first_half}.get(dist, ())
-            if dist:
+            passed = [
+                chunk
+                for step in program for y_at, *acts in step if y_at == who
+                for kind, which, _, order in acts if kind == "pass" and which == l
+                for chunk in order
+            ]
+            order = tuple(chunk for chunk in forward if chunk not in passed)
+            if who != own and order:
                 at_y(who, functools.partial(w_wait, l, order))
         if l % OWN == 0:
             at_y(own, own_w.wait)
@@ -258,7 +247,7 @@
                     ready[l, r, pl.ds((p * 4 + i) * BLOCK, BLOCK), :] = part.astype(jnp.bfloat16)
             return carry
 
-        lax.fori_loop(0, BD, one, 0)
+        lax.fori_loop(0, BD, one, 0, unroll=4)
 
         line_left = lax.broadcasted_iota(jnp.int32, (1, 128), 1) < BLOCK
 
@@ -268,56 +257,64 @@
             bias_tiles[l, pl.ds(2 * p, 1), :] = jnp.where(line_left, row, turn)
             bias_tiles[l, pl.ds(2 * p + 1, 1), :] = jnp.where(line_left, turn, row)
 
-    def leaf(l, s, u, dx, dz, dc, part):
-        tiles = pl.ds(u * 16 + part[0], part[1])
+    def leaf(l, s, u, dx, dz, dc, at, n):
+        tiles = pl.ds(u * 16 + at, n)
         return pltpu.make_async_remote_copy(
             stage.at[l, s, tiles], land[l][s].at[tiles], leaf_send.at[l, s], leaf_recv.at[l, s],
             device_id=device(0, dx, dz, dc), device_id_type=MESH,
         )
 
-    def spread(l, s):
+    def hop_wait(l, s):
         pltpu.make_async_remote_copy(
-            cur[l][s].at[pl.ds(1, 2)], cur[l][s].at[pl.ds(1, 2)], hop_send.at[l, s], hop_recv.at[l, s],
+            near[l][s], near[l][s], hop_send.at[l, s], hop_recv.at[l, s],
             device_id=device(0, 0, 2, 0), device_id_type=MESH,
         ).wait_recv()
 
+    def columns(l, s, parts, far):
         def column(t, carry):
             dx = (t // 2) ^ 2
             dc = t % 2
             u = dx * 2 + dc
             cc = (c + dc) % C
             xx = ((x + dx) % X) * Z
-
-            def put(at, q, dz):
-                for k in range(2):
-                    index = stab[l // OWN, l % OWN, xx + (z + dz + Z) % Z, 4 * q + 2 * cc + k]
-                    stage[l, s, u * 16 + at + k] = cur[l][s][q, index]
-
-            far = 2 - 4 * dc
-            put(14, 1 + dc, far)
-            leaf(l, s, u, dx, far, dc, FAR).start()
-            put(6, 0, 1)
-            put(8, 1, 1)
-            leaf(l, s, u, dx, 1, dc, AHEAD).start()
-            put(10, 0, -1)
-            put(12, 2, -1)
-            leaf(l, s, u, dx, -1, dc, BACK).start()
-            put(0, 0, 0)
-            put(2, 1, 0)
-            put(4, 2, 0)
-
-            @pl.when(u > 0)
-            def _():
-                leaf(l, s, u, dx, 0, dc, NEAR).start()
-
+            todo = parts
+            if far:
+                todo = ((14, 2 - 4 * dc, (1 + dc,)),) + parts
+            moves = []
+            for at, dz, sources in todo:
+                for i, q in enumerate(sources):
+                    for k in range(2):
+                        index = stab[l // OWN, l % OWN, xx + (z + dz + Z) % Z, 4 * q + 2 * cc + k]
+                        moves.append((u * 16 + at + 2 * i + k, q, index))
+            tiles = [near[l][s][q - 1, i] if far else cur[l][s][i] for _, q, i in moves]
+            for (at, _, _), tile in zip(moves, tiles):
+                stage[l, s, at] = tile
+            for at, dz, sources in todo:
+                go = leaf(l, s, u, dx, dz, dc, at, 2 * len(sources))
+                if isinstance(dz, int) and dz == 0:
+                    pl.when(u > 0)(go.start)
+                else:
+                    go.start()
             return carry
 
         lax.fori_loop(0, X * C, column, 0)
-        for k in range(NEAR[1]):
-            land[l][s][k] = stage[l, s, k]
+        for at, dz, sources in parts:
+            if dz == 0:
+                for k in range(at, at + 2 * len(sources)):
+                    land[l][s][k] = stage[l, s, k]
+
+    def pack_own(l, s):
+        columns(l, s, OWN_PARTS, False)
+
+    def pack(l, s):
+        columns(l, s, RELAY_PARTS, True)
+
+    def spread(l, s):
+        hop_wait(l, s)
+        pack(l, s)
 
     def gather(l, s):
-        tiles = pl.ds(NEAR[1], 8 * 16 - NEAR[1])
+        tiles = pl.ds(HERE, 8 * 16 - HERE)
         pltpu.make_async_remote_copy(
             stage.at[l, s, tiles], land[l][s].at[tiles], leaf_send.at[l, s], leaf_recv.at[l, s],
             device_id=device(0, 1, 0, 0), device_id_type=MESH,
@@ -332,17 +329,23 @@
 
     def advance(l, s):
         gather(l, s)
-
+        compute(l, s)
+        start_hops(l + 1, s)
+        pack_own(l + 1, s)
+
+    def compute(l, s):
         def pair(p, carry):
             for r in range(2):
-                cur[l + 1][s][0, 2 * p + r] = block_out(l, s, 2 * p + r).astype(jnp.bfloat16)
+                cur[l + 1][s][2 * p + r] = block_out(l, s, 2 * p + r).astype(jnp.bfloat16)
             return carry
 
-        lax.fori_loop(0, BD // 2, pair, 0)
-        start_hops(l + 1, s)
+        lax.fori_loop(0, BD // 2, pair, 0, unroll=8)
 
     def finish(l, s):
         gather(l, s)
+        finish_compute(l, s)
+
+    def finish_compute(l, s):
         half = left[:rs]
 
         def pair(p, carry):
@@ -354,7 +357,22 @@
             out_ref[pl.ds(16 + s * rs, rs), cols] = high.astype(jnp.bfloat16)
             return carry
 
-        lax.fori_loop(0, BD // 2, pair, 0)
+        lax.fori_loop(0, BD // 2, pair, 0, unroll=8)
+
+    def tab_wait(who):
+        @pl.when(y != who)
+        def _():
+            pltpu.make_async_remote_copy(
+                tabs.at[who], tabs.at[who], tab_send, tab_recv.at[who],
+                device_id=device(1, 0, 0, 0), device_id_type=MESH,
+            ).wait_recv()
+
+    def to_smem(l):
+        at = (l // OWN, l % OWN)
+        return pltpu.make_async_copy(tabs.at[at], stab.at[at], smem_sem.at[l])
+
+    def smem_wait(l):
+        to_smem(l).wait()
 
     for dy in (2, 1, 3):
         tab_copy(dy).start()
@@ -363,58 +381,77 @@
     for dy in (1, 2, 3):
         bias_copy(dy).start()
     point(0)
-    pltpu.make_async_remote_copy(
-        tabs.at[pl.ds(0, 3)], tabs.at[pl.ds(0, 3)], tab_send, tab_recv,
-        device_id=device(1, 0, 0, 0), device_id_type=MESH,
-    ).wait()
-    to_smem = pltpu.make_async_copy(tabs, stab, local_sem.at[1])
-    to_smem.start()
-    to_smem.wait()
-
-    last = LAYERS - 1
-    spread(0, 0)
-    spread(0, 1)
-    point(1)
+    tab_wait(0)
+    to_smem(0).start()
+    to_smem(1).start()
+    smem_wait(0)
+    for s in range(SUBS):
+        pack_own(0, s)
+    for s in range(SUBS):
+        spread(0, s)
+    for who in range(1, PIPE):
+        tab_wait(who)
+        for a in range(OWN):
+            to_smem(who * OWN + a).start()
     pltpu.make_async_remote_copy(
         biases.at[pl.ds(0, 3)], biases.at[pl.ds(0, 3)], bias_send, bias_recv,
         device_id=device(1, 0, 0, 0), device_id_type=MESH,
     ).wait()
+    point(1)
     arrive(0)
     prepare(0)
-    for l in range(LAYERS):
+    last = LAYERS - 1
+    order = [(l, s) for l in range(LAYERS) for s in range(SUBS)]
+    lag = 1 if SUBS > 2 else 0
+    for n, (l, s) in enumerate(order):
+        if s == 0 and l < last:
+            smem_wait(l + 1)
         if l < last:
-            advance(l, 0)
-            spread(l + 1, 0)
-            advance(l, 1)
+            advance(l, s)
+        else:
+            finish(l, s)
+        late = l == 0
+        if s == SUBS - 1 and l < last:
             point(l + 2)
-            if l == 0:
-                spread(l + 1, 1)
+            if not late:
+                arrive(l + 1)
+                prepare(l + 1)
+        if n >= lag:
+            behind_l, behind_s = order[n - lag]
+            if behind_l < last:
+                spread(behind_l + 1, behind_s)
+        if s == SUBS - 1 and late:
             arrive(l + 1)
             prepare(l + 1)
-            if l > 0:
-                spread(l + 1, 1)
-        else:
-            finish(l, 0)
-            finish(l, 1)
-
+
+    pltpu.make_async_remote_copy(
+        tabs.at[pl.ds(0, 3)], tabs.at[pl.ds(0, 3)], tab_send, tab_recv.at[0],
+        device_id=device(1, 0, 0, 0), device_id_type=MESH,
+    ).wait_send()
     for l in range(LAYERS):
         for s in range(SUBS):
             pltpu.make_async_remote_copy(
-                cur[l][s].at[pl.ds(0, 2)], cur[l][s].at[pl.ds(0, 2)], hop_send.at[l, s], hop_recv.at[l, s],
+                near[l][s], near[l][s], hop_send.at[l, s], hop_recv.at[l, s],
                 device_id=device(0, 0, 2, 0), device_id_type=MESH,
             ).wait_send()
-            tiles = pl.ds(NEAR[1], 8 * 16 - NEAR[1])
+            tiles = pl.ds(HERE, 8 * 16 - HERE)
             pltpu.make_async_remote_copy(
                 stage.at[l, s, tiles], land[l][s].at[tiles], leaf_send.at[l, s], leaf_recv.at[l, s],
                 device_id=device(0, 1, 0, 0), device_id_type=MESH,
             ).wait_send()
     for who in range(PIPE):
-        n = {0: 4 + 1, 1: 4 + 1, 2: 6 + 1, 3: 6 + 1}[who]
+        pieces = sum(
+            len(order) * len(ways)
+            for step in program for y_at, *acts in step if y_at == who
+            for _, _, ways, order in acts
+        )
 
         @functools.partial(at_y, who)
         def _():
             pltpu.make_async_remote_copy(
-                wall.at[pl.ds(0, n)], wall.at[pl.ds(0, n)], w_send, w_recv.at[0, 0],
+                wall.at[:, pl.ds(0, pieces * rows // LAYERS)],
+                wall.at[:, pl.ds(0, pieces * rows // LAYERS)],
+                w_send, w_recv.at[0, 0],
                 device_id=device(1, 0, 0, 0), device_id_type=MESH,
             ).wait_send()
 
@@ -440,12 +477,14 @@
             pltpu.VMEM((LAYERS, BD, 2 * BLOCK), jnp.float32),
             pltpu.VMEM((PIPE, OWN, ROWS // 2 + 8, 128), jnp.int32),
             pltpu.SMEM((PIPE, OWN, ROWS // 2 + 8, 128), jnp.int32),
-            [[pltpu.VMEM((3, BD, rs, 128), jnp.bfloat16)] * SUBS] * LAYERS,
+            [[pltpu.VMEM((BD, rs, 128), jnp.bfloat16)] * SUBS] * LAYERS,
+            [[pltpu.VMEM((2, BD, rs, 128), jnp.bfloat16)] * SUBS] * LAYERS,
             pltpu.VMEM((LAYERS, SUBS, 128, rs, 128), jnp.bfloat16),
             [[pltpu.VMEM((128, rs, 128), jnp.bfloat16)] * SUBS] * LAYERS,
-            pltpu.SemaphoreType.DMA((2,)),
+            pltpu.SemaphoreType.DMA((1,)),
+            pltpu.SemaphoreType.DMA((LAYERS,)),
             pltpu.SemaphoreType.DMA,
-            pltpu.SemaphoreType.DMA,
+            pltpu.SemaphoreType.DMA((PIPE,)),
             pltpu.SemaphoreType.DMA,
             pltpu.SemaphoreType.DMA,
             pltpu.SemaphoreType.DMA,
@@ -458,7 +497,7 @@
         compiler_params=pltpu.CompilerParams(
             collective_id=0, has_side_effects=True, vmem_limit_bytes=60 * 1024 * 1024
         ),
-    )(features, weights, bias, layout.reshape(OWN, ROWS // 2, 128))
+    )(features, weights, bias, layout)
 
 
 def solution(mesh):

time: 134 us -> 120 us (0.90)
  the two profiles are of different devices: /device:TPU:24 before, /device:TPU:16 now
where the time goes in v2:
time: 120 us
  Pallas kernels  118 us (98%)
  local copies, waits for them, and re-layouts  1.47 us (1%)
    pallas_call x1, Pallas kernels, on_device(): pl.pallas_call(kernel, name='sections', out_shape=jax.ShapeDtypeStruct(fe...  118 us

profile of v2, /device:TPU:16, one launch (start us, length us, event | category | flops | bytes accessed | tf_op | source)
XLA Modules:
  0.0 119.7 jit_solution(16167698388080321245)
XLA Ops:
  0.0 118.2 %sections.1 = bf16[32,1024]{1,0:T(8,128)(2,1)} custom-call(bf16[32,1024]{1,0:T(8,128)(2,1)} %feat_ref.1, bf16[2,16,64,256]{3,2,1,0:T(8,128)(2,1)} %w_hbm.1, bf16[2,1024]{1,0:T(2,128)(2,1)} %bias_ref.1, s32[2,4096]{1,0:T(2,128)} %lay_ref.1), custom_call_target="tpu_custom_call" | custom-call | tf_op jit(solution)/shard_map/sections/pallas_call | solution.py:462
  118.2 1.5 %copy.6 = bf16[32,1024]{1,0:T(8,128)(2,1)} copy(bf16[32,1024]{1,0:T(8,128)(2,1)} %sections.1) | data formatting | bytes 131072

commit v3 on v2

--- a/solution.py
+++ b/solution.py
@@ -16,7 +16,8 @@
 LAYERS = 8
 OWN = LAYERS // PIPE
 BD = 16
-SUBS = 2
+SUBS = 4
+LAG = 1
 CHUNKS = 4
 clamp_top = 32.0
 
@@ -27,13 +28,13 @@
 
 def place():
     me = lax.axis_index("rows")
-    return lax.axis_index("pipe"), me // (Z * C), (me // C) % Z, me % C
+    return lax.axis_index("pipe"), me >> 4, (me >> 1) & (Z - 1), me & (C - 1)
 
 
 def device(dy, dx, dz, dc):
     y, x, z, c = place()
-    row = (((x + dx + X) % X) * Z + (z + dz + Z) % Z) * C + (c + dc) % C
-    return ((y + dy + PIPE) % PIPE, row)
+    row = (((x + dx) & (X - 1)) << 4) | (((z + dz) & (Z - 1)) << 1) | ((c ^ dc) & (C - 1))
+    return ((y + dy) & (PIPE - 1), row)
 
 
 def offsets():
@@ -94,16 +95,16 @@
         )
         owner = entry >> 4
         key = slot * BD + (entry & 15)
-        table = jnp.zeros((ROWS // 2, 128), jnp.int32)
-        for q, dz in enumerate((0, -2, 2)):
-            source = (x * Z + (z + dz + Z) % Z) * C + c
-            for half in range(2):
+        for half in range(2):
+            table = jnp.zeros((ROWS // 2, 128), jnp.int32)
+            for q, dz in enumerate((0, -2, 2)):
+                source = (x << 4) | (((z + dz) & (Z - 1)) << 1) | c
                 hit = (owner == source) & ((lane >> 6) == half)
                 first = jnp.min(jnp.where(hit, key, 1 << 20), axis=1, keepdims=True) & 15
                 last = jnp.max(jnp.where(hit, key, 0), axis=1, keepdims=True) & 15
-                table = jnp.where(lane == 4 * q + 2 * half, first, table)
-                table = jnp.where(lane == 4 * q + 2 * half + 1, last, table)
-        tabs[y, a, pl.ds(0, ROWS // 2)] = table
+                table = jnp.where(lane == 2 * q, first, table)
+                table = jnp.where(lane == 2 * q + 1, last, table)
+            tabs[y, a, pl.ds(half * ROWS // 2, ROWS // 2)] = table
     mine = jnp.concatenate(
         [lay_ref[:, pl.ds(pl.multiple_of((x * Z + z) * 128, 128), 128)]]
         + [jnp.zeros((8 - OWN, 128), jnp.int32)],
@@ -123,7 +124,10 @@
         base = jnp.where(dz == d, at, base)
     where = (dx * 2 + dc) * 16 + base + rank
     for a in range(OWN):
-        tabs[y, a, pl.ds(ROWS // 2, 8)] = jnp.broadcast_to(where[a : a + 1], (8, 128))
+        both_rows = jnp.concatenate(
+            [where[a : a + 1], pltpu.roll(where, 64, 1)[a : a + 1], jnp.zeros((6, 128), jnp.int32)], axis=0
+        )
+        tabs[y, a, pl.ds(ROWS, 8)] = both_rows
 
     with jax.named_scope("barrier_wait"):
         pl.semaphore_wait(barrier, len(partners))
@@ -175,61 +179,69 @@
     def at_y(which, act):
         pl.when(y == which)(act)
 
-    first_half, last_half, forward, turned = (0, 1), (2, 3), (0, 1, 2, 3), (2, 3, 0, 1)
-
-    both, ahead, behind = (1, -1), (1,), (-1,)
-    program = (
-        (
-            (0, ("own", 0, both, forward), ("own", 1, both, forward)),
-            (1, ("own", 0, behind, turned), ("own", 1, behind, turned)),
-            (2, ("own", 0, both, forward), ("own", 1, both, forward)),
-            (3, ("own", 0, ahead, forward), ("own", 1, ahead, forward)),
+
+    h1, h2 = (0, 1), (2, 3)
+
+    def own(which, *ways):
+        return tuple(
+            ("own", which, dy, chunks or (h1 + h2 if dy > 0 else h2 + h1)) for dy, chunks in ways
+        )
+
+    def fwd(l, dy, chunks):
+        return (("pass", l, dy, chunks),)
+
+    up, down = (1, None), (-1, None)
+    program = {
+        "start": (
+            (0, own(0, up, down)),
+            (1, own(0, down) + own(1, down)),
+            (2, own(0, up, down) + own(1, up, down)),
+            (3, own(0, up) + own(1, up)),
         ),
-        (
-            (1, ("pass", 0, ahead, first_half), ("own", 0, ahead, forward), ("own", 1, ahead, forward)),
-            (3, ("pass", 0, behind, last_half)),
+        "first": ((0, own(1, up, down)), (1, fwd(0, 1, h1)), (3, fwd(0, -1, h2))),
+        (0, 1): ((1, fwd(1, 1, (0,))), (3, fwd(1, -1, (2,)))),
+        (0, 2): ((1, fwd(1, 1, (1,)) + own(0, (1, h1))), (3, fwd(1, -1, (3,)))),
+        (0, 3): ((0, fwd(2, -1, h2) + fwd(3, -1, h2)),),
+        (1, 0): ((1, own(1, (1, h1))),),
+        (1, 1): ((2, fwd(2, 1, (0,))), (3, fwd(2, -1, (2,)))),
+        (1, 3): ((2, fwd(2, 1, (1,))), (3, fwd(2, -1, (3,)))),
+        (2, 0): ((2, fwd(3, 1, h1)),),
+        (2, 1): (
+            (0, fwd(6, 1, h1) + fwd(7, 1, h1)),
+            (1, fwd(4, -1, h2) + fwd(5, -1, h2)),
+            (3, fwd(3, -1, h2) + fwd(4, 1, h1) + fwd(5, 1, h1)),
         ),
-        (
-            (0, ("pass", 2, behind, last_half), ("pass", 3, behind, last_half)),
-            (2, ("pass", 2, ahead, first_half)),
-            (3, ("pass", 1, behind, forward), ("own", 0, behind, turned), ("own", 1, behind, turned)),
-        ),
-        (
-            (0, ("pass", 6, ahead, first_half), ("pass", 7, ahead, first_half)),
-            (1, ("pass", 4, behind, last_half), ("pass", 5, behind, last_half)),
-            (2, ("pass", 3, ahead, first_half)),
-            (3, ("pass", 4, ahead, first_half), ("pass", 5, ahead, first_half)),
-        ),
-        (
-            (2, ("pass", 6, behind, last_half), ("pass", 7, behind, last_half)),
-        ),
-    )
-
-    def point(p):
-        for who, *acts in program[p] if p < len(program) else ():
+        (2, 3): ((3, own(0, down) + own(1, down)),),
+        (4, 0): ((2, fwd(6, -1, h2)),),
+        (5, 0): ((2, fwd(7, -1, h2)),),
+    }
+
+    def acts_of(who):
+        return [act for step in program.values() for y_at, acts in step if y_at == who for act in acts]
+
+    def point(*at):
+        for who, acts in program.get(at if len(at) > 1 else at[0], ()):
             @functools.partial(at_y, who)
             def _():
-                for kind, which, ways, order in acts:
-                    for dy in ways:
-                        if kind == "own":
-                            w_own(which, dy, order)
-                        else:
-                            w_pass(which, order, dy)
+                for kind, which, dy, order in acts:
+                    if kind == "own":
+                        w_own(which, dy, order)
+                    else:
+                        w_pass(which, order, dy)
 
     def arrive(l):
-        own = l // OWN
+        owner = l // OWN
         for who in range(PIPE):
             passed = [
                 chunk
-                for step in program for y_at, *acts in step if y_at == who
-                for kind, which, _, order in acts if kind == "pass" and which == l
+                for kind, which, _, order in acts_of(who) if kind == "pass" and which == l
                 for chunk in order
             ]
-            order = tuple(chunk for chunk in forward if chunk not in passed)
-            if who != own and order:
+            order = tuple(chunk for chunk in h1 + h2 if chunk not in passed)
+            if who != owner and order:
                 at_y(who, functools.partial(w_wait, l, order))
         if l % OWN == 0:
-            at_y(own, own_w.wait)
+            at_y(owner, own_w.wait)
 
     def prepare(l):
         keep = lax.broadcasted_iota(jnp.int32, (BLOCK, 128), 1) < BLOCK
@@ -257,8 +269,8 @@
             bias_tiles[l, pl.ds(2 * p, 1), :] = jnp.where(line_left, row, turn)
             bias_tiles[l, pl.ds(2 * p + 1, 1), :] = jnp.where(line_left, turn, row)
 
-    def leaf(l, s, u, dx, dz, dc, at, n):
-        tiles = pl.ds(u * 16 + at, n)
+    def leaf(l, s, base, dx, dz, dc, at, n):
+        tiles = pl.ds(base + at, n)
         return pltpu.make_async_remote_copy(
             stage.at[l, s, tiles], land[l][s].at[tiles], leaf_send.at[l, s], leaf_recv.at[l, s],
             device_id=device(0, dx, dz, dc), device_id_type=MESH,
@@ -272,32 +284,35 @@
 
     def columns(l, s, parts, far):
         def column(t, carry):
-            dx = (t // 2) ^ 2
-            dc = t % 2
-            u = dx * 2 + dc
-            cc = (c + dc) % C
-            xx = ((x + dx) % X) * Z
-            todo = parts
-            if far:
-                todo = ((14, 2 - 4 * dc, (1 + dc,)),) + parts
+            dx = t ^ 2
+            xx = ((x + dx) & (X - 1)) << 3
+            plans = []
+            for dc in range(C):
+                todo = parts
+                if far:
+                    todo = ((14, 2 - 4 * dc, (1 + dc,)),) + parts
+                plans.append((dc, (dx * 2 + dc) * 16, todo))
             moves = []
-            for at, dz, sources in todo:
-                for i, q in enumerate(sources):
-                    for k in range(2):
-                        index = stab[l // OWN, l % OWN, xx + (z + dz + Z) % Z, 4 * q + 2 * cc + k]
-                        moves.append((u * 16 + at + 2 * i + k, q, index))
+            for dc, base, todo in plans:
+                for at, dz, sources in todo:
+                    row = ((c ^ dc) << 5) | xx | ((z + dz) & (Z - 1))
+                    for i, q in enumerate(sources):
+                        for k in range(2):
+                            index = stab[l // OWN, l % OWN, row, 2 * q + k]
+                            moves.append((base + at + 2 * i + k, q, index))
             tiles = [near[l][s][q - 1, i] if far else cur[l][s][i] for _, q, i in moves]
             for (at, _, _), tile in zip(moves, tiles):
                 stage[l, s, at] = tile
-            for at, dz, sources in todo:
-                go = leaf(l, s, u, dx, dz, dc, at, 2 * len(sources))
-                if isinstance(dz, int) and dz == 0:
-                    pl.when(u > 0)(go.start)
-                else:
-                    go.start()
+            for dc, base, todo in plans:
+                for at, dz, sources in todo:
+                    go = leaf(l, s, base, dx, dz, dc, at, 2 * len(sources))
+                    if dz == 0 and dc == 0:
+                        pl.when(dx > 0)(go.start)
+                    else:
+                        go.start()
             return carry
 
-        lax.fori_loop(0, X * C, column, 0)
+        lax.fori_loop(0, X, column, 0)
         for at, dz, sources in parts:
             if dz == 0:
                 for k in range(at, at + 2 * len(sources)):
@@ -321,8 +336,8 @@
         ).wait_recv()
 
     def block_out(l, s, r):
-        row = stab.at[l // OWN, l % OWN, ROWS // 2]
-        lhs = jnp.concatenate([land[l][s][row[c * 64 + r * K + k]] for k in range(K)], axis=1)
+        row = stab.at[l // OWN, l % OWN, ROWS + c]
+        lhs = jnp.concatenate([land[l][s][row[r * K + k]] for k in range(K)], axis=1)
         total = jnp.dot(lhs, ready[l, r], preferred_element_type=jnp.float32)
         total = total + bias_tiles[l, pl.ds(r, 1), :]
         return jnp.minimum(jnp.maximum(total, 0.0), clamp_top)
@@ -380,7 +395,7 @@
         start_hops(0, s)
     for dy in (1, 2, 3):
         bias_copy(dy).start()
-    point(0)
+    point("start")
     tab_wait(0)
     to_smem(0).start()
     to_smem(1).start()
@@ -397,12 +412,11 @@
         biases.at[pl.ds(0, 3)], biases.at[pl.ds(0, 3)], bias_send, bias_recv,
         device_id=device(1, 0, 0, 0), device_id_type=MESH,
     ).wait()
-    point(1)
+    point("first")
     arrive(0)
     prepare(0)
     last = LAYERS - 1
     order = [(l, s) for l in range(LAYERS) for s in range(SUBS)]
-    lag = 1 if SUBS > 2 else 0
     for n, (l, s) in enumerate(order):
         if s == 0 and l < last:
             smem_wait(l + 1)
@@ -410,17 +424,15 @@
             advance(l, s)
         else:
             finish(l, s)
-        late = l == 0
-        if s == SUBS - 1 and l < last:
-            point(l + 2)
-            if not late:
-                arrive(l + 1)
-                prepare(l + 1)
-        if n >= lag:
-            behind_l, behind_s = order[n - lag]
+        point(l, s)
+        if s == SUBS - 1 and 0 < l < last:
+            arrive(l + 1)
+            prepare(l + 1)
+        if n >= LAG:
+            behind_l, behind_s = order[n - LAG]
             if behind_l < last:
                 spread(behind_l + 1, behind_s)
-        if s == SUBS - 1 and late:
+        if s == SUBS - 1 and l == 0:
             arrive(l + 1)
             prepare(l + 1)
 
@@ -440,11 +452,7 @@
                 device_id=device(0, 1, 0, 0), device_id_type=MESH,
             ).wait_send()
     for who in range(PIPE):
-        pieces = sum(
-            len(order) * len(ways)
-            for step in program for y_at, *acts in step if y_at == who
-            for _, _, ways, order in acts
-        )
+        pieces = sum(len(order) for _, _, _, order in acts_of(who))
 
         @functools.partial(at_y, who)
         def _():
@@ -475,8 +483,8 @@
             pltpu.VMEM((LAYERS, BD, 2 * K * BLOCK, 2 * BLOCK), jnp.bfloat16),
             pltpu.VMEM((PIPE, OWN, n), jnp.bfloat16),
             pltpu.VMEM((LAYERS, BD, 2 * BLOCK), jnp.float32),
-            pltpu.VMEM((PIPE, OWN, ROWS // 2 + 8, 128), jnp.int32),
-            pltpu.SMEM((PIPE, OWN, ROWS // 2 + 8, 128), jnp.int32),
+            pltpu.VMEM((PIPE, OWN, ROWS + 8, 128), jnp.int32),
+            pltpu.SMEM((PIPE, OWN, ROWS + 8, 128), jnp.int32),
             [[pltpu.VMEM((BD, rs, 128), jnp.bfloat16)] * SUBS] * LAYERS,
             [[pltpu.VMEM((2, BD, rs, 128), jnp.bfloat16)] * SUBS] * LAYERS,
             pltpu.VMEM((LAYERS, SUBS, 128, rs, 128), jnp.bfloat16),

time: 120 us -> 110 us (0.917)
  the two profiles are of different devices: /device:TPU:16 before, /device:TPU:24 now
where the time goes in v3:
time: 110 us; the launch traced here: 109 us
  Pallas kernels  107 us (97%)
  local copies, waits for them, and re-layouts  1.47 us (1%)
    pallas_call x1, Pallas kernels, on_device(): pl.pallas_call(kernel, name='sections', out_shape=jax.ShapeDtypeStruct(fe...  107 us

profile of v3, /device:TPU:24, one launch (start us, length us, event | category | flops | bytes accessed | tf_op | source)
XLA Modules:
  0.0 108.7 jit_solution(13786248345234919486)
XLA Ops:
  0.0 107.2 %sections.1 = bf16[32,1024]{1,0:T(8,128)(2,1)} custom-call(bf16[32,1024]{1,0:T(8,128)(2,1)} %feat_ref.1, bf16[2,16,64,256]{3,2,1,0:T(8,128)(2,1)} %w_hbm.1, bf16[2,1024]{1,0:T(2,128)(2,1)} %bias_ref.1, s32[2,4096]{1,0:T(2,128)} %lay_ref.1), custom_call_target="tpu_custom_call" | custom-call | tf_op jit(solution)/shard_map/sections/pallas_call | solution.py:470
  107.3 1.5 %copy.6 = bf16[32,1024]{1,0:T(8,128)(2,1)} copy(bf16[32,1024]{1,0:T(8,128)(2,1)} %sections.1) | data formatting | bytes 131072

commit v4 on v3

--- a/solution.py
+++ b/solution.py
@@ -129,12 +129,13 @@
         )
         tabs[y, a, pl.ds(ROWS, 8)] = both_rows
 
+    own_w.wait()
     with jax.named_scope("barrier_wait"):
         pl.semaphore_wait(barrier, len(partners))
 
-    def tab_copy(dy):
+    def tab_copy(a, dy):
         return pltpu.make_async_remote_copy(
-            tabs.at[y], tabs.at[y], tab_send, tab_recv.at[y],
+            tabs.at[y, a], tabs.at[y, a], tab_send, tab_recv.at[y, a],
             device_id=device(dy, 0, 0, 0), device_id_type=MESH,
         )
 
@@ -165,7 +166,7 @@
 
     def w_own(a, dy, order):
         for chunk in order:
-            w_copy(OWN * y + a, chunk, dy, w_hbm.at[a]).start()
+            w_copy(OWN * y + a, chunk, dy, wall.at[OWN * y + a]).start()
 
     def w_wait(l, order):
         for chunk in order:
@@ -195,25 +196,21 @@
         "start": (
             (0, own(0, up, down)),
             (1, own(0, down) + own(1, down)),
-            (2, own(0, up, down) + own(1, up, down)),
+            (2, own(0, down) + own(1, down)),
             (3, own(0, up) + own(1, up)),
         ),
-        "first": ((0, own(1, up, down)), (1, fwd(0, 1, h1)), (3, fwd(0, -1, h2))),
-        (0, 1): ((1, fwd(1, 1, (0,))), (3, fwd(1, -1, (2,)))),
-        (0, 2): ((1, fwd(1, 1, (1,)) + own(0, (1, h1))), (3, fwd(1, -1, (3,)))),
-        (0, 3): ((0, fwd(2, -1, h2) + fwd(3, -1, h2)),),
-        (1, 0): ((1, own(1, (1, h1))),),
-        (1, 1): ((2, fwd(2, 1, (0,))), (3, fwd(2, -1, (2,)))),
-        (1, 3): ((2, fwd(2, 1, (1,))), (3, fwd(2, -1, (3,)))),
-        (2, 0): ((2, fwd(3, 1, h1)),),
-        (2, 1): (
-            (0, fwd(6, 1, h1) + fwd(7, 1, h1)),
-            (1, fwd(4, -1, h2) + fwd(5, -1, h2)),
-            (3, fwd(3, -1, h2) + fwd(4, 1, h1) + fwd(5, 1, h1)),
+        "first": ((1, fwd(0, 1, h1) + own(0, (1, h1))), (3, fwd(0, -1, h2))),
+        (0, 0): ((0, own(1, up, down)), (1, fwd(1, 1, (0,))), (3, fwd(1, -1, (2,)))),
+        (0, 1): (
+            (1, fwd(1, 1, (1,)) + own(0, (1, h2)) + own(1, up)),
+            (3, fwd(1, -1, (3,)) + own(0, down) + own(1, down)),
         ),
-        (2, 3): ((3, own(0, down) + own(1, down)),),
-        (4, 0): ((2, fwd(6, -1, h2)),),
-        (5, 0): ((2, fwd(7, -1, h2)),),
+        (0, 2): ((2, fwd(2, 1, h1) + own(0, up)),),
+        (0, 3): ((0, fwd(2, -1, h2)),),
+        (1, 0): ((0, fwd(3, -1, h2)), (1, fwd(4, -1, h1 + h2) + fwd(5, -1, h1 + h2))),
+        (2, 0): ((2, fwd(3, 1, h1) + own(1, up)),),
+        (2, 1): ((0, fwd(6, 1, h1) + fwd(7, 1, h1)), (2, fwd(6, -1, h2))),
+        (3, 0): ((2, fwd(7, -1, h2)),),
     }
 
     def acts_of(who):
@@ -240,8 +237,6 @@
             order = tuple(chunk for chunk in h1 + h2 if chunk not in passed)
             if who != owner and order:
                 at_y(who, functools.partial(w_wait, l, order))
-        if l % OWN == 0:
-            at_y(owner, own_w.wait)
 
     def prepare(l):
         keep = lax.broadcasted_iota(jnp.int32, (BLOCK, 128), 1) < BLOCK
@@ -374,11 +369,12 @@
 
         lax.fori_loop(0, BD // 2, pair, 0, unroll=8)
 
-    def tab_wait(who):
-        @pl.when(y != who)
+    def tab_wait(l):
+        @pl.when(y != l // OWN)
         def _():
+            at = (l // OWN, l % OWN)
             pltpu.make_async_remote_copy(
-                tabs.at[who], tabs.at[who], tab_send, tab_recv.at[who],
+                tabs.at[at], tabs.at[at], tab_send, tab_recv.at[at],
                 device_id=device(1, 0, 0, 0), device_id_type=MESH,
             ).wait_recv()
 
@@ -390,24 +386,24 @@
         to_smem(l).wait()
 
     for dy in (2, 1, 3):
-        tab_copy(dy).start()
+        tab_copy(0, dy).start()
     for s in range(SUBS):
         start_hops(0, s)
+    for dy in (2, 1, 3):
+        tab_copy(1, dy).start()
     for dy in (1, 2, 3):
         bias_copy(dy).start()
     point("start")
     tab_wait(0)
     to_smem(0).start()
-    to_smem(1).start()
     smem_wait(0)
     for s in range(SUBS):
         pack_own(0, s)
     for s in range(SUBS):
         spread(0, s)
-    for who in range(1, PIPE):
-        tab_wait(who)
-        for a in range(OWN):
-            to_smem(who * OWN + a).start()
+    for l in range(1, LAYERS):
+        tab_wait(l)
+        to_smem(l).start()
     pltpu.make_async_remote_copy(
         biases.at[pl.ds(0, 3)], biases.at[pl.ds(0, 3)], bias_send, bias_recv,
         device_id=device(1, 0, 0, 0), device_id_type=MESH,
@@ -437,7 +433,7 @@
             prepare(l + 1)
 
     pltpu.make_async_remote_copy(
-        tabs.at[pl.ds(0, 3)], tabs.at[pl.ds(0, 3)], tab_send, tab_recv.at[0],
+        tabs.at[pl.ds(0, 3)], tabs.at[pl.ds(0, 3)], tab_send, tab_recv.at[0, 0],
         device_id=device(1, 0, 0, 0), device_id_type=MESH,
     ).wait_send()
     for l in range(LAYERS):
@@ -492,7 +488,7 @@
             pltpu.SemaphoreType.DMA((1,)),
             pltpu.SemaphoreType.DMA((LAYERS,)),
             pltpu.SemaphoreType.DMA,
-            pltpu.SemaphoreType.DMA((PIPE,)),
+            pltpu.SemaphoreType.DMA((PIPE, OWN)),
             pltpu.SemaphoreType.DMA,
             pltpu.SemaphoreType.DMA,
             pltpu.SemaphoreType.DMA,

time: 110 us -> 107 us (0.973)
  Pallas kernels: 107 us -> 104 us
    pallas_call x1, Pallas kernels: 107 us -> 104 us  [on_device(): pl.pallas_call(kernel, name='sections', out_shape=jax.ShapeDtypeStruct(fe...]
where the time goes in v4:
time: 107 us; the launch traced here: 106 us
  Pallas kernels  104 us (97%)
  local copies, waits for them, and re-layouts  1.47 us (1%)
    pallas_call x1, Pallas kernels, on_device(): pl.pallas_call(kernel, name='sections', out_shape=jax.ShapeDtypeStruct(fe...  104 us

profile of v4, /device:TPU:24, one launch (start us, length us, event | category | flops | bytes accessed | tf_op | source)
XLA Modules:
  0.0 105.8 jit_solution(11778576284809058256)
XLA Ops:
  0.0 104.3 %sections.1 = bf16[32,1024]{1,0:T(8,128)(2,1)} custom-call(bf16[32,1024]{1,0:T(8,128)(2,1)} %feat_ref.1, bf16[2,16,64,256]{3,2,1,0:T(8,128)(2,1)} %w_hbm.1, bf16[2,1024]{1,0:T(2,128)(2,1)} %bias_ref.1, s32[2,4096]{1,0:T(2,128)} %lay_ref.1), custom_call_target="tpu_custom_call" | custom-call | tf_op jit(solution)/shard_map/sections/pallas_call | solution.py:466
  104.4 1.5 %copy.6 = bf16[32,1024]{1,0:T(8,128)(2,1)} copy(bf16[32,1024]{1,0:T(8,128)(2,1)} %sections.1) | data formatting | bytes 131072

commit v5 on v4

--- a/solution.py
+++ b/solution.py
@@ -17,7 +17,6 @@
 OWN = LAYERS // PIPE
 BD = 16
 SUBS = 4
-LAG = 1
 CHUNKS = 4
 clamp_top = 32.0
 
@@ -199,17 +198,22 @@
             (2, own(0, down) + own(1, down)),
             (3, own(0, up) + own(1, up)),
         ),
-        "first": ((1, fwd(0, 1, h1) + own(0, (1, h1))), (3, fwd(0, -1, h2))),
-        (0, 0): ((0, own(1, up, down)), (1, fwd(1, 1, (0,))), (3, fwd(1, -1, (2,)))),
+        "first": (
+            (0, own(1, up, down)),
+            (1, fwd(0, 1, h1) + own(0, (1, h1))),
+            (3, fwd(0, -1, h2)),
+        ),
+        (0, 0): ((1, fwd(1, 1, (0,))), (3, fwd(1, -1, (2,)))),
         (0, 1): (
             (1, fwd(1, 1, (1,)) + own(0, (1, h2)) + own(1, up)),
             (3, fwd(1, -1, (3,)) + own(0, down) + own(1, down)),
         ),
-        (0, 2): ((2, fwd(2, 1, h1) + own(0, up)),),
+        (0, 2): ((2, fwd(2, 1, h1) + own(0, (1, h1))),),
         (0, 3): ((0, fwd(2, -1, h2)),),
         (1, 0): ((0, fwd(3, -1, h2)), (1, fwd(4, -1, h1 + h2) + fwd(5, -1, h1 + h2))),
-        (2, 0): ((2, fwd(3, 1, h1) + own(1, up)),),
-        (2, 1): ((0, fwd(6, 1, h1) + fwd(7, 1, h1)), (2, fwd(6, -1, h2))),
+        (1, 3): ((2, fwd(3, 1, (0,))),),
+        (2, 0): ((2, fwd(3, 1, (1,)) + own(0, (1, h2))),),
+        (2, 1): ((0, fwd(6, 1, h1) + fwd(7, 1, h1)), (2, own(1, up) + fwd(6, -1, h2))),
         (3, 0): ((2, fwd(7, -1, h2)),),
     }
 
@@ -412,25 +416,22 @@
     arrive(0)
     prepare(0)
     last = LAYERS - 1
-    order = [(l, s) for l in range(LAYERS) for s in range(SUBS)]
-    for n, (l, s) in enumerate(order):
-        if s == 0 and l < last:
-            smem_wait(l + 1)
-        if l < last:
+    for l in range(LAYERS):
+        if l == last:
+            for s in range(SUBS):
+                finish(l, s)
+            break
+        smem_wait(l + 1)
+        for s in range(SUBS):
             advance(l, s)
-        else:
-            finish(l, s)
-        point(l, s)
-        if s == SUBS - 1 and 0 < l < last:
-            arrive(l + 1)
-            prepare(l + 1)
-        if n >= LAG:
-            behind_l, behind_s = order[n - LAG]
-            if behind_l < last:
-                spread(behind_l + 1, behind_s)
-        if s == SUBS - 1 and l == 0:
-            arrive(l + 1)
-            prepare(l + 1)
+        point(l, 0)
+        point(l, 1)
+        for s in range(SUBS):
+            spread(l + 1, s)
+        point(l, 2)
+        point(l, 3)
+        arrive(l + 1)
+        prepare(l + 1)
 
     pltpu.make_async_remote_copy(
         tabs.at[pl.ds(0, 3)], tabs.at[pl.ds(0, 3)], tab_send, tab_recv.at[0, 0],

time: 107 us -> 102 us (0.953); the launches traced: 106 us -> 102 us
  Pallas kernels: 104 us -> 100 us
    pallas_call x1, Pallas kernels: 104 us -> 100 us  [on_device(): pl.pallas_call(kernel, name='sections', out_shape=jax.ShapeDtypeStruct(fe...]
where the time goes in v5:
time: 102 us
  Pallas kernels  100 us (98%)
  local copies, waits for them, and re-layouts  1.47 us (1%)
    pallas_call x1, Pallas kernels, on_device(): pl.pallas_call(kernel, name='sections', out_shape=jax.ShapeDtypeStruct(fe...  100 us

profile of v5, /device:TPU:24, one launch (start us, length us, event | category | flops | bytes accessed | tf_op | source)
XLA Modules:
  0.0 101.9 jit_solution(3566254684735236894)
XLA Ops:
  0.0 100.4 %sections.1 = bf16[32,1024]{1,0:T(8,128)(2,1)} custom-call(bf16[32,1024]{1,0:T(8,128)(2,1)} %feat_ref.1, bf16[2,16,64,256]{3,2,1,0:T(8,128)(2,1)} %w_hbm.1, bf16[2,1024]{1,0:T(2,128)(2,1)} %bias_ref.1, s32[2,4096]{1,0:T(2,128)} %lay_ref.1), custom_call_target="tpu_custom_call" | custom-call | tf_op jit(solution)/shard_map/sections/pallas_call | solution.py:467
  100.4 1.5 %copy.6 = bf16[32,1024]{1,0:T(8,128)(2,1)} copy(bf16[32,1024]{1,0:T(8,128)(2,1)} %sections.1) | data formatting | bytes 131072

commit v6 on v5

--- a/solution.py
+++ b/solution.py
@@ -281,7 +281,7 @@
             device_id=device(0, 0, 2, 0), device_id_type=MESH,
         ).wait_recv()
 
-    def columns(l, s, parts, far):
+    def columns(l, s, parts, relay, far):
         def column(t, carry):
             dx = t ^ 2
             xx = ((x + dx) & (X - 1)) << 3
@@ -299,7 +299,7 @@
                         for k in range(2):
                             index = stab[l // OWN, l % OWN, row, 2 * q + k]
                             moves.append((base + at + 2 * i + k, q, index))
-            tiles = [near[l][s][q - 1, i] if far else cur[l][s][i] for _, q, i in moves]
+            tiles = [near[l][s][q - 1, i] if relay else cur[l][s][i] for _, q, i in moves]
             for (at, _, _), tile in zip(moves, tiles):
                 stage[l, s, at] = tile
             for dc, base, todo in plans:
@@ -318,10 +318,11 @@
                     land[l][s][k] = stage[l, s, k]
 
     def pack_own(l, s):
-        columns(l, s, OWN_PARTS, False)
+        columns(l, s, OWN_PARTS, False, False)
 
     def pack(l, s):
-        columns(l, s, RELAY_PARTS, True)
+        columns(l, s, RELAY_PARTS[:2], True, True)
+        columns(l, s, RELAY_PARTS[2:], True, False)
 
     def spread(l, s):
         hop_wait(l, s)

time: 102 us -> 102 us (level)
  no operation moved by 1% of the time
where the time goes in v6:
time: 102 us
  Pallas kernels  100 us (98%)
  local copies, waits for them, and re-layouts  1.47 us (1%)
    pallas_call x1, Pallas kernels, on_device(): pl.pallas_call(kernel, name='sections', out_shape=jax.ShapeDtypeStruct(fe...  100 us

profile of v6, /device:TPU:24, one launch (start us, length us, event | category | flops | bytes accessed | tf_op | source)
XLA Modules:
  0.0 101.9 jit_solution(17639990669762426235)
XLA Ops:
  0.0 100.5 %sections.1 = bf16[32,1024]{1,0:T(8,128)(2,1)} custom-call(bf16[32,1024]{1,0:T(8,128)(2,1)} %feat_ref.1, bf16[2,16,64,256]{3,2,1,0:T(8,128)(2,1)} %w_hbm.1, bf16[2,1024]{1,0:T(2,128)(2,1)} %bias_ref.1, s32[2,4096]{1,0:T(2,128)} %lay_ref.1), custom_call_target="tpu_custom_call" | custom-call | tf_op jit(solution)/shard_map/sections/pallas_call | solution.py:468
  100.5 1.5 %copy.6 = bf16[32,1024]{1,0:T(8,128)(2,1)} copy(bf16[32,1024]{1,0:T(8,128)(2,1)} %sections.1) | data formatting | bytes 131072
